TPU v7x, 32 devices: a whole 2x2x4 slice. The times are simulated.
32 devices in a mesh: tm: 16 (over z, x, core), rows: 2 (over y).
Axes of the slice: x: 2, y: 2, z: 4, core: 2. Of those that a mesh axis runs over, the one named last changes fastest.
Arguments:
- observations: float32 [32, 16, 1024], P('tm', 'rows'), may hold values from -6 to 6
- obs_noise: float32 [32, 16, 1024], P('tm', 'rows'), may hold values from -6 to 6
- prior_noise: float32 [32, 16, 1024], P('tm', 'rows'), may hold values from -4.8 to 4.8
- observed: int32 [32, 16, 1024], P('tm', 'rows'), may hold values 0 or 1
- kappa_sq: float32 [16, 1024], P('rows'), may hold values from 0.5 to 8
- obs_precision: float32 [16, 1024], P('rows'), may hold values from 0.2 to 2
Outputs:
- solution: float32 [32, 16, 1024], P('tm', 'rows')
- residual: float32 [32, 16, 1024], P('tm', 'rows')
- precond: float32 [32, 16, 1024], P('tm', 'rows')
All inputs are finite; a program needn't handle non-finite values. No bound on the sum of `observed` on one device may be relied on, other than what follows from the above.
Results may differ from a plain program's by a relative error of at most 0.002.
Values sent between devices are 32-bit elements; how exact they have to be, the bound alone decides.
No kernel may reach another device: no remote copies, remote signals or barrier semaphores. Data moves between devices by JAX's collectives and lax.ppermute only.
A program may use at most 64 MiB of HBM per device.

v0:
```python
import jax
import jax.numpy as jnp
from jax import lax
from jax.sharding import PartitionSpec as P

ITERS = 2


coupling = 0.995


def with_halo(array, sides, width):
    for axis, dim in sides:
        devices, length = (lax.axis_size(axis), array.shape[dim])
        up = [(i, (i + 1) % devices) for i in range(devices - 1)]
        down = [(j, i) for i, j in up]
        last = lax.slice_in_dim(array, length - width, length, axis=dim)
        initial = lax.slice_in_dim(array, 0, width, axis=dim)
        before = lax.ppermute(last, axis, up)
        after = lax.ppermute(initial, axis, down)
        array = jnp.concatenate([before, array, after], axis=dim)
    return array


def carried_in(value, axis, join, neutral, backward):
    count, mine = (lax.axis_size(axis), lax.axis_index(axis))
    pieces = jax.tree.map(lambda part: lax.all_gather(part, axis), value)
    if backward:
        pieces = jax.tree.map(lambda part: part[::-1], pieces)
        mine = count - 1 - mine
    so_far = jax.tree.map(
        lambda part, zero: jnp.full_like(part, 0) + jnp.asarray(zero, part.dtype), value, neutral
    )

    def turn(position, so_far):
        longer = join(so_far, jax.tree.map(lambda part: part[position], pieces))
        return jax.tree.map(lambda new, old: jnp.where(position < mine, new, old), longer, so_far)

    return lax.fori_loop(0, count - 1, turn, so_far)


def mat_combine(earlier, later):
    e_upper_left, e_upper_right, e_lower_left, e_lower_right = earlier
    l_upper_left, l_upper_right, l_lower_left, l_lower_right = later
    new_ul = l_upper_left * e_upper_left + l_upper_right * e_lower_left
    new_ur = l_upper_left * e_upper_right + l_upper_right * e_lower_right
    new_ll = l_lower_left * e_upper_left + l_lower_right * e_lower_left
    new_lr = l_lower_left * e_upper_right + l_lower_right * e_lower_right
    largest = jnp.maximum(
        jnp.maximum(jnp.abs(new_ul), jnp.abs(new_ur)), jnp.maximum(jnp.abs(new_ll), jnp.abs(new_lr))
    )
    return (new_ul / largest, new_ur / largest, new_ll / largest, new_lr / largest)


def affine_combine(earlier, later):
    return (later[0] * earlier[0], later[0] * earlier[1] + later[1])


def local_product(main_diagonal_entries, offdiagonal_entries):
    unit_field = jnp.ones_like(offdiagonal_entries)
    empty_field_grid = jnp.zeros_like(offdiagonal_entries)

    def local_advance(current_state, main_row):
        factor_now = (empty_field_grid, offdiagonal_entries, -offdiagonal_entries, main_row)
        return (mat_combine(current_state, factor_now), None)

    state_end, unused_item = lax.scan(
        local_advance,
        (unit_field, empty_field_grid, empty_field_grid, unit_field),
        main_diagonal_entries,
        reverse=False,
    )
    return state_end


def pivots(main_diagonal_entries, offdiagonal_entries, ratio_start):

    def pivots_advance(previous_ratio, main_row):
        pivot_entry = main_row - offdiagonal_entries * previous_ratio
        current_ratio = offdiagonal_entries / pivot_entry
        return (current_ratio, (previous_ratio, pivot_entry, current_ratio))

    unused_item, (ratio_before, pivot_rows, ratio_rows) = lax.scan(
        pivots_advance, ratio_start, main_diagonal_entries, reverse=False
    )
    return (ratio_before, pivot_rows, ratio_rows)


def apply_affine_scan(decay_rate, source, backward):

    def apply_advance(value_prev, matrix_entries):
        rate_row, forcing_row = matrix_entries
        current_value = rate_row * value_prev + forcing_row
        return (current_value, current_value)

    unused_item, value_list = lax.scan(
        apply_advance, jnp.zeros_like(source[0]), (decay_rate, source), reverse=backward
    )
    return value_list


def reverse_cumprod(value_list):
    return jnp.flip(jnp.cumprod(jnp.flip(value_list, 0), axis=0), 0)


def operate(field, stencil_diag, weights, obs_weight):
    padded = with_halo(field, (("rows", 1),), 1)
    column_zero = jnp.zeros_like(field[:, :, :1])
    left_part = jnp.concatenate([column_zero, field[:, :, :-1]], axis=2)
    right_side = jnp.concatenate([field[:, :, 1:], column_zero], axis=2)
    beside = padded[:, 2:] + padded[:, :-2] + right_side + left_part
    spatial = stencil_diag * field - beside
    hour_pad = with_halo(spatial, (("tm", 0),), 1)
    return weights * spatial - coupling * (hour_pad[2:] + hour_pad[:-2]) + obs_weight * field


def inner_total(value_list):
    return lax.psum(jnp.sum(value_list), ("tm", "rows"))


def curve_total(value_list):
    return lax.psum(jnp.sum(value_list), ("tm", "rows"))


def per_device(observations, obs_noise, prior_noise, observed, kappa_sq, obs_precision):
    hour_block = observations.shape[0]
    maskf = observed.astype(jnp.float32)
    obs_weight = maskf * obs_precision
    right = (
        maskf * (obs_precision * observations + jnp.sqrt(obs_precision) * obs_noise) + prior_noise
    )
    stencil_diag = kappa_sq + 4.0
    hour_count = hour_block * lax.axis_size("tm")
    global_hour = lax.axis_index("tm") * hour_block + jnp.arange(hour_block, dtype=jnp.int32)
    boundary = (global_hour == 0) | (global_hour == hour_count - 1)
    weights = jnp.where(boundary, 1.0, 1.0 + coupling * coupling).astype(jnp.float32)[:, None, None]
    main_diagonal_entries = weights * stencil_diag + obs_weight
    offdiagonal_entries = -coupling * stencil_diag
    unit_field = jnp.ones_like(offdiagonal_entries)
    empty_field_grid = jnp.zeros_like(offdiagonal_entries)
    identity_mat = (unit_field, empty_field_grid, empty_field_grid, unit_field)
    front_pair = carried_in(
        local_product(main_diagonal_entries, offdiagonal_entries),
        "tm",
        mat_combine,
        identity_mat,
        False,
    )
    ratio_start = front_pair[1] / front_pair[3]
    ratio_before, pivot_rows, ratio_rows = pivots(
        main_diagonal_entries, offdiagonal_entries, ratio_start
    )
    decay_rate = -offdiagonal_entries / pivot_rows
    rate_cum = jnp.cumprod(decay_rate, axis=0)

    def forward_solve(right_hand_part):
        partial_result = apply_affine_scan(decay_rate, right_hand_part / pivot_rows, False)
        incoming = carried_in(
            (rate_cum[-1], partial_result[-1]),
            "tm",
            affine_combine,
            (unit_field, empty_field_grid),
            False,
        )
        return (partial_result + rate_cum * incoming[1], incoming[1])

    sweep_factor = -ratio_rows
    cum_sweep = reverse_cumprod(sweep_factor)

    def solve(right_hand_part):
        leading_elimination, unused_item = forward_solve(right_hand_part)
        partial_result = apply_affine_scan(sweep_factor, leading_elimination, True)
        incoming = carried_in(
            (cum_sweep[0], partial_result[0]),
            "tm",
            affine_combine,
            (unit_field, empty_field_grid),
            True,
        )
        return partial_result + cum_sweep * incoming[1]

    solution = jnp.zeros_like(right)
    residual = right
    precond = solve(residual)
    direction = precond
    aligned = inner_total(residual * precond)
    for iteration in range(ITERS):
        applied = operate(direction, stencil_diag, weights, obs_weight)
        step_size = aligned / curve_total(direction * applied)
        solution = solution + step_size * direction
        residual = residual - step_size * applied
        precond = solve(residual)
        aligned_new = inner_total(residual * precond)
        direction = precond + aligned_new / aligned * direction
        aligned = aligned_new
    return (solution, residual, precond)


def solution(mesh):
    in_specs = (
        P("tm", "rows", None),
        P("tm", "rows", None),
        P("tm", "rows", None),
        P("tm", "rows", None),
        P("rows", None),
        P("rows", None),
    )
    out_specs = (P("tm", "rows", None), P("tm", "rows", None), P("tm", "rows", None))
    return jax.shard_map(
        per_device, mesh=mesh, in_specs=in_specs, out_specs=out_specs, check_vma=False
    )
```

profile of v0, /device:TPU:0, one launch (start us, length us, event | category | flops | bytes accessed | tf_op | source)
XLA Modules:
  0.0 413.0 jit_solution(10433346282122587190)
XLA Ops:
  3.2 24.6 %all-gather = f32[128,1024]{1,0:T(8,128)S(1)} all-gather(f32[8,1024]{1,0:T(8,128)S(1)} %get-tuple-element.1233), channel_id=2, replica_groups=mesh['tm'=16,'rows'=2] {'tm'}, dimensions={0}, use_global_device_ids=true | all-gather | bytes 557056 | tf_op jit(solution)/shard_map/all_gather | solution.py:27
  27.8 18.9 %all-gather.1 = f32[128,1024]{1,0:T(8,128)S(1)} all-gather(f32[8,1024]{1,0:T(8,128)S(1)} %get-tuple-element.1234), channel_id=3, replica_groups=mesh['tm'=16,'rows'=2] {'tm'}, dimensions={0}, use_global_device_ids=true | all-gather | bytes 557056 | tf_op jit(solution)/shard_map/all_gather | solution.py:27
  46.7 20.3 %all-gather.2 = f32[128,1024]{1,0:T(8,128)S(1)} all-gather(f32[8,1024]{1,0:T(8,128)S(1)} %get-tuple-element.1235), channel_id=4, replica_groups=mesh['tm'=16,'rows'=2] {'tm'}, dimensions={0}, use_global_device_ids=true | all-gather | bytes 557056 | tf_op jit(solution)/shard_map/all_gather | solution.py:27
  67.0 18.9 %all-gather.3 = f32[128,1024]{1,0:T(8,128)S(1)} all-gather(f32[8,1024]{1,0:T(8,128)S(1)} %get-tuple-element.1236), channel_id=5, replica_groups=mesh['tm'=16,'rows'=2] {'tm'}, dimensions={0}, use_global_device_ids=true | all-gather | bytes 557056 | tf_op jit(solution)/shard_map/all_gather | solution.py:27
  85.8 1.5 while.228
  89.0 20.3 %all_gather.61 = f32[16,8,1024]{2,1,0:T(8,128)S(1)} all-gather(f32[1,8,1024]{2,1,0:T(8,128)S(1)} %slice.98), channel_id=1, replica_groups=mesh['tm'=16,'rows'=2] {'tm'}, dimensions={0}, use_global_device_ids=true | all-gather | bytes 557056 | tf_op jit(solution)/shard_map/all_gather | solution.py:27
  109.3 18.9 %all_gather.60 = f32[16,8,1024]{2,1,0:T(8,128)S(1)} all-gather(f32[1,8,1024]{2,1,0:T(8,128)S(1)} %slice.125), channel_id=1, replica_groups=mesh['tm'=16,'rows'=2] {'tm'}, dimensions={0}, use_global_device_ids=true | all-gather | bytes 557056 | tf_op jit(solution)/shard_map/all_gather | solution.py:27
  128.9 20.3 %all_gather.63 = f32[16,8,1024]{2,1,0:T(8,128)S(1)} all-gather(f32[1,8,1024]{2,1,0:T(8,128)S(1)} %slice.100), channel_id=1, replica_groups=mesh['tm'=16,'rows'=2] {'tm'}, dimensions={0}, use_global_device_ids=true | all-gather | bytes 557056 | tf_op jit(solution)/shard_map/all_gather | solution.py:27
  149.7 18.9 %all_gather.62 = f32[16,8,1024]{2,1,0:T(8,128)S(1)} all-gather(f32[1,8,1024]{2,1,0:T(8,128)S(1)} %slice.126), channel_id=1, replica_groups=mesh['tm'=16,'rows'=2] {'tm'}, dimensions={0}, use_global_device_ids=true | all-gather | bytes 557056 | tf_op jit(solution)/shard_map/all_gather | solution.py:27
  169.4 1.3 collective-permute-start
  170.7 4.5 %collective-permute-start.1 = (f32[2,1,1024]{2,1,0:T(1,128)S(1)}, f32[2,1,1024]{2,1,0:T(1,128)S(1)}, u32[]{:S(2)}, u32[]{:S(2)}) collective-permute-start(f32[2,1,1024]{2,1,0:T(1,128)S(1)} %get-tuple-element.1752), channel_id=1, source_target_pairs={{0,1},{2,3},{4,5},{6,7},{8,9},{10,11},{12,13},{14,15},{16,17},{18,... | collective-permute-start | bytes 24584 | tf_op jit(solution)/shard_map/ppermute | solution.py:19
  176.7 1.3 collective-permute-start.2
  178.0 3.0 collective-permute-start.3
  182.5 42.8 %all-reduce.4 = (f32[]{:T(128)}, f32[]{:T(128)}) all-reduce(f32[]{:T(128)} %get-tuple-element.1530, f32[]{:T(128)} %get-tuple-element.1529), channel_id=1, replica_groups=mesh['tm'=16,'rows'=2] {'tm','rows'}, use_global_device_ids=true, to_apply=%region_17.18 | all-reduce | flops 2 | bytes 16 | tf_op jit(solution)/shard_map/psum | solution.py:118
  226.8 21.8 %all_gather.64 = f32[16,8,1024]{2,1,0:T(8,128)S(1)} all-gather(f32[1,8,1024]{2,1,0:T(8,128)S(1)} %slice.111), channel_id=1, replica_groups=mesh['tm'=16,'rows'=2] {'tm'}, dimensions={0}, use_global_device_ids=true | all-gather | bytes 557056 | tf_op jit(solution)/shard_map/all_gather | solution.py:27
  249.3 18.9 %all_gather.65 = f32[16,8,1024]{2,1,0:T(8,128)S(1)} all-gather(f32[1,8,1024]{2,1,0:T(8,128)S(1)} %slice.112), channel_id=1, replica_groups=mesh['tm'=16,'rows'=2] {'tm'}, dimensions={0}, use_global_device_ids=true | all-gather | bytes 557056 | tf_op jit(solution)/shard_map/all_gather | solution.py:27
  269.5 38.9 %psum.30 = f32[]{:T(128)} all-reduce(f32[]{:T(128)} %multiply_reduce_fusion.1), channel_id=1, replica_groups=mesh['tm'=16,'rows'=2] {'tm','rows'}, use_global_device_ids=true, to_apply=%region_29.30 | all-reduce | flops 1 | bytes 8 | tf_op jit(solution)/shard_map/psum | solution.py:118
  309.8 1.3 collective-permute-start.4
  311.1 4.5 %collective-permute-start.5 = (f32[2,1,1024]{2,1,0:T(1,128)S(1)}, f32[2,1,1024]{2,1,0:T(1,128)S(1)}, u32[]{:S(2)}, u32[]{:S(2)}) collective-permute-start(f32[2,1,1024]{2,1,0:T(1,128)S(1)} %get-tuple-element.1746), channel_id=1, source_target_pairs={{0,1},{2,3},{4,5},{6,7},{8,9},{10,11},{12,13},{14,15},{16,17},{18,... | collective-permute-start | bytes 24584 | tf_op jit(solution)/shard_map/ppermute | solution.py:19
  317.1 1.3 collective-permute-start.6
  318.4 3.0 collective-permute-start.7
  323.0 45.2 %psum.31 = f32[]{:T(128)} all-reduce(f32[]{:T(128)} %get-tuple-element.1727), channel_id=1, replica_groups=mesh['tm'=16,'rows'=2] {'tm','rows'}, use_global_device_ids=true, to_apply=%region_31.32 | all-reduce | flops 1 | bytes 8 | tf_op jit(solution)/shard_map/psum | solution.py:122
  370.3 21.8 %all_gather.66 = f32[16,8,1024]{2,1,0:T(8,128)S(1)} all-gather(f32[1,8,1024]{2,1,0:T(8,128)S(1)} %slice.123), channel_id=1, replica_groups=mesh['tm'=16,'rows'=2] {'tm'}, dimensions={0}, use_global_device_ids=true | all-gather | bytes 557056 | tf_op jit(solution)/shard_map/all_gather | solution.py:27
  392.8 18.9 %all_gather.67 = f32[16,8,1024]{2,1,0:T(8,128)S(1)} all-gather(f32[1,8,1024]{2,1,0:T(8,128)S(1)} %slice.124), channel_id=1, replica_groups=mesh['tm'=16,'rows'=2] {'tm'}, dimensions={0}, use_global_device_ids=true | all-gather | bytes 557056 | tf_op jit(solution)/shard_map/all_gather | solution.py:27
  (241 shorter events, 19.2 us)
Async XLA Ops:
  0.6 0.8 copy-start.5
  1.4 0.8 copy-start.1
  2.1 0.8 copy-start
  87.4 0.8 copy-start.2
  87.4 0.9 copy-start.3
  87.5 0.9 copy-start.4
  169.4 5.9 %collective-permute-start = (f32[2,1,1024]{2,1,0:T(1,128)S(1)}, f32[2,1,1024]{2,1,0:T(1,128)S(1)}, u32[]{:S(2)}, u32[]{:S(2)}) collective-permute-start(f32[2,1,1024]{2,1,0:T(1,128)S(1)} %get-tuple-element.1751), channel_id=1, source_target_pairs={{1,0},{3,2},{5,4},{7,6},{9,8},{11,10},{13,12},{15,14},{17,16},{19,... | collective-permute-start | bytes 24584 | tf_op jit(solution)/shard_map/ppermute | solution.py:20
  170.7 5.9 %collective-permute-start.1 = (f32[2,1,1024]{2,1,0:T(1,128)S(1)}, f32[2,1,1024]{2,1,0:T(1,128)S(1)}, u32[]{:S(2)}, u32[]{:S(2)}) collective-permute-start(f32[2,1,1024]{2,1,0:T(1,128)S(1)} %get-tuple-element.1752), channel_id=1, source_target_pairs={{0,1},{2,3},{4,5},{6,7},{8,9},{10,11},{12,13},{14,15},{16,17},{18,... | collective-permute-start | bytes 24584 | tf_op jit(solution)/shard_map/ppermute | solution.py:19
  176.7 4.4 %collective-permute-start.2 = (f32[1,8,1024]{2,1,0:T(8,128)S(1)}, f32[1,8,1024]{2,1,0:T(8,128)S(1)}, u32[]{:S(2)}, u32[]{:S(2)}) collective-permute-start(f32[1,8,1024]{2,1,0:T(8,128)S(1)} %get-tuple-element.1747), channel_id=1, source_target_pairs={{2,0},{4,2},{6,4},{8,6},{10,8},{12,10},{14,12},{16,14},{18,16},{20... | collective-permute-start | bytes 98312 | tf_op jit(solution)/shard_map/ppermute | solution.py:20
  178.0 3.9 collective-permute-start.3
  309.8 5.9 %collective-permute-start.4 = (f32[2,1,1024]{2,1,0:T(1,128)S(1)}, f32[2,1,1024]{2,1,0:T(1,128)S(1)}, u32[]{:S(2)}, u32[]{:S(2)}) collective-permute-start(f32[2,1,1024]{2,1,0:T(1,128)S(1)} %get-tuple-element.1745), channel_id=1, source_target_pairs={{1,0},{3,2},{5,4},{7,6},{9,8},{11,10},{13,12},{15,14},{17,16},{19,... | collective-permute-start | bytes 24584 | tf_op jit(solution)/shard_map/ppermute | solution.py:20
  311.1 5.9 %collective-permute-start.5 = (f32[2,1,1024]{2,1,0:T(1,128)S(1)}, f32[2,1,1024]{2,1,0:T(1,128)S(1)}, u32[]{:S(2)}, u32[]{:S(2)}) collective-permute-start(f32[2,1,1024]{2,1,0:T(1,128)S(1)} %get-tuple-element.1746), channel_id=1, source_target_pairs={{0,1},{2,3},{4,5},{6,7},{8,9},{10,11},{12,13},{14,15},{16,17},{18,... | collective-permute-start | bytes 24584 | tf_op jit(solution)/shard_map/ppermute | solution.py:19
  317.1 4.4 %collective-permute-start.6 = (f32[1,8,1024]{2,1,0:T(8,128)S(1)}, f32[1,8,1024]{2,1,0:T(8,128)S(1)}, u32[]{:S(2)}, u32[]{:S(2)}) collective-permute-start(f32[1,8,1024]{2,1,0:T(8,128)S(1)} %get-tuple-element.1741), channel_id=1, source_target_pairs={{2,0},{4,2},{6,4},{8,6},{10,8},{12,10},{14,12},{16,14},{18,16},{20... | collective-permute-start | bytes 98312 | tf_op jit(solution)/shard_map/ppermute | solution.py:20
  318.4 3.9 collective-permute-start.7
where the time goes:
time: 414 us; the launch traced here: 413 us
  blocking collectives  369 us (89%)
  starting transfers between devices  20.3 us (5%)
  other arithmetic  7.23 us (2%)
  between operations  5.35 us (1%)
    all_gather x12, blocking collectives, carried_in(): pieces = jax.tree.map(lambda part: lax.all_gather(part, axis), value)  242 us
    psum x2, blocking collectives, inner_total(): return lax.psum(jnp.sum(value_list), ('tm', 'rows'))  81.7 us
    psum x1, blocking collectives, curve_total(): return lax.psum(jnp.sum(value_list), ('tm', 'rows'))  45.2 us
    ppermute x4, starting transfers between devices, with_halo(): before = lax.ppermute(last, axis, up)  15.1 us
  transfers between devices with their start and end apart: 8, of which 4 were waited for; matrix products, arithmetic and copies ran while one was open for 0% of the time, Pallas kernels for 0%

commit v1 on v0

v1 whole, which is shorter than its diff:
```python
import jax
import jax.numpy as jnp
from jax import lax
from jax.sharding import PartitionSpec as P

ITERS = 2
coupling = 0.995
AXES = ("tm", "rows")


def column_windows(field, blocks, halo):
    width = field.shape[-1] // blocks
    split = field.shape[:-1] + (blocks, width)
    parts = []
    for step in range(halo, 0, -1):
        moved = jnp.pad(field, [(0, 0)] * (field.ndim - 1) + [(step, 0)])[..., : field.shape[-1]]
        parts.append(moved.reshape(split)[..., :1])
    parts.append(field.reshape(split))
    for step in range(1, halo + 1):
        moved = jnp.pad(field, [(0, 0)] * (field.ndim - 1) + [(0, step)])[..., step:]
        parts.append(moved.reshape(split)[..., -1:])
    return jnp.concatenate(parts, axis=-1)


def hour_factors(main, off):
    def advance(inverse, row):
        inverse = 1.0 / (row - off * off * inverse)
        return inverse, inverse

    return lax.scan(advance, jnp.zeros_like(off), main)[1]


def hour_solve(right, inverse, ratio):
    def down(before, entries):
        value, inv, rat = entries
        now = value * inv - rat * before
        return now, now

    def up(after, entries):
        value, rat = entries
        now = value - rat * after
        return now, now

    zero = jnp.zeros_like(right[0])
    forward = lax.scan(down, zero, (right, inverse, ratio))[1]
    return lax.scan(up, zero, (forward, ratio), reverse=True)[1]


def split_off(field, weights):
    padded = jnp.pad(field, ((0, 0), (1, 1), (1, 1)))
    beside = padded[:, 2:, 1:-1] + padded[:, :-2, 1:-1] + padded[:, 1:-1, 2:] + padded[:, 1:-1, :-2]
    hours = jnp.pad(beside, ((1, 1), (0, 0), (0, 0)))
    return weights * beside - coupling * (hours[2:] + hours[:-2])


def step_scalars(a, h, hp, k, m, n):
    alpha = a / (a - h)
    delta = -h / (a - h)
    rz = delta * delta * a + alpha * delta * (h + hp) + alpha * alpha * k
    g = delta + rz / a
    curve = g * g * (a - h) + g * alpha * (h - m + hp - k) + alpha * alpha * (k - n)
    beta = rz / curve
    return alpha + beta * g, beta * alpha, delta - beta * g, alpha + beta * g - beta * alpha


def per_device(observations, obs_noise, prior_noise, observed, kappa_sq, obs_precision):
    hours, rows, columns = observations.shape
    over_tm, over_rows = lax.axis_size("tm"), lax.axis_size("rows")
    blocks = over_tm * over_rows
    width = columns // blocks
    wide = width + 2 * ITERS
    mask = observed.astype(jnp.float32)
    obs_weight = mask * obs_precision
    right = (
        mask * (obs_precision * observations + jnp.sqrt(obs_precision) * obs_noise) + prior_noise
    )
    payload = jnp.concatenate([right, obs_weight, kappa_sq[None]], axis=0)
    payload = jnp.moveaxis(column_windows(payload, blocks, ITERS), 2, 0)
    payload = payload.reshape(blocks, -1)
    got = lax.all_to_all(payload, AXES, split_axis=0, concat_axis=0, tiled=True)
    got = got.reshape(over_tm, over_rows, 2 * hours + 1, rows, wide)
    got = jnp.moveaxis(got, 2, 1)
    all_rows = over_rows * rows
    every = over_tm * hours
    r0 = got[:, :hours].reshape(every, all_rows, wide)
    ow = got[:, hours : 2 * hours].reshape(every, all_rows, wide)
    diag = got[0, 2 * hours].reshape(all_rows, wide) + 4.0
    where = (lax.axis_index("tm") * over_rows + lax.axis_index("rows")) * width
    column = where - ITERS + jnp.arange(wide, dtype=jnp.int32)
    inside = (column >= 0) & (column < columns)
    hour = jnp.arange(every)
    ends = (hour == 0) | (hour == every - 1)
    weights = jnp.where(ends, 1.0, 1.0 + coupling * coupling).astype(jnp.float32)[:, None, None]
    off = -coupling * diag
    inverse = hour_factors(weights * diag + ow, off)
    ratio = off * inverse
    z0 = hour_solve(r0, inverse, ratio)
    s1 = jnp.where(inside, split_off(z0, weights), 0.0)
    y1 = hour_solve(s1, inverse, ratio)
    s2 = jnp.where(inside, split_off(y1, weights), 0.0)
    y2 = hour_solve(s2, inverse, ratio)
    own = slice(ITERS, ITERS + width)
    r0, z0, s1, y1, s2, y2 = (part[:, :, own] for part in (r0, z0, s1, y1, s2, y2))
    pairs = ((r0, z0), (z0, s1), (r0, y1), (s1, y1), (z0, s2), (y1, s2))
    sums = jnp.stack([jnp.sum(x * y) for x, y in pairs])
    back = jnp.stack([z0, y1, y2, s1, s2]).reshape(-1, over_tm, hours, over_rows, rows, width)
    items = back.shape[0]
    back = back.transpose(1, 3, 0, 2, 4, 5).reshape(blocks, -1)
    back = jnp.concatenate([back, jnp.broadcast_to(sums, (blocks, sums.shape[0]))], axis=1)
    got = lax.all_to_all(back, AXES, split_axis=0, concat_axis=0, tiled=True)
    sums = jnp.sum(got[:, -sums.shape[0] :], axis=0)
    got = got[:, : -sums.shape[0]].reshape(blocks, items, hours, rows, width)
    z0, y1, y2, s1, s2 = got.transpose(1, 2, 3, 0, 4).reshape(items, hours, rows, columns)
    cx, c2, c0, c1 = step_scalars(*sums)
    return (
        cx * z0 + c2 * y1,
        c0 * right + c1 * s1 + c2 * s2,
        c0 * z0 + c1 * y1 + c2 * y2,
    )


def solution(mesh):
    whole, plane = P("tm", "rows", None), P("rows", None)
    return jax.shard_map(
        per_device,
        mesh=mesh,
        in_specs=(whole, whole, whole, whole, plane, plane),
        out_specs=(whole, whole, whole),
        check_vma=False,
    )
```

time: 414 us -> 75.5 us (0.18)
  blocking collectives: 369 us -> 13.7 us
  local copies, waits for them, and re-layouts: 3.44 us -> 21.4 us
  starting transfers between devices: 20.3 us -> 7.33 us
  waiting for transfers between devices: 4.12 us -> 9.53 us
  between operations: 5.35 us -> 10.7 us
    all_gather x12 -> x0, blocking collectives: 242 us -> none  [carried_in(): pieces = jax.tree.map(lambda part: lax.all_gather(part, axis), value)]
    psum x3 -> x0, blocking collectives: 127 us -> none  [the longest x2 81.7 us: inner_total(): return lax.psum(jnp.sum(value_list), ('tm', 'rows'))]
    ppermute x8 -> x0, starting transfers between devices: 20.3 us -> none  [the longest x4 15.1 us: with_halo(): before = lax.ppermute(last, axis, up)]
    all_to_all x0 -> x1, blocking collectives: none -> 13.7 us  [per_device(): got = lax.all_to_all(back, AXES, split_axis=0, concat_axis=0, tiled=True)]
    all_to_all x0 -> x1, waiting for transfers between devices: none -> 9.53 us  [per_device(): got = lax.all_to_all(payload, AXES, split_axis=0, concat_axis=0, tiled=True)]
    all_to_all x0 -> x1, starting transfers between devices: none -> 7.33 us  [per_device(): got = lax.all_to_all(payload, AXES, split_axis=0, concat_axis=0, tiled=True)]
    concatenate x0 -> x8, local copies, waits for them, and re-layouts: none -> 6.26 us  [the longest x6 4.47 us: per_device(): payload = jnp.concatenate([right, obs_weight, kappa_sq[None]], axis=0)]
    another operation x8 -> x11, local copies, waits for them, and re-layouts: 0.05 us -> 4.78 us  [the longest x1 3.88 us: per_device(): sums = jnp.stack([jnp.sum(x * y) for x, y in pairs])]
  transfers between devices with their start and end apart: 8 -> 1, of which waited for: 4 -> 1; matrix products, arithmetic and copies ran while one was open for 0% -> 0% of each run, Pallas kernels for 0% -> 0%
where the time goes in v1:
time: 75.5 us; the launch traced here: 74.9 us
  local copies, waits for them, and re-layouts  21.4 us (28%)
  blocking collectives  13.7 us (18%)
  between operations  10.7 us (14%)
  waiting for transfers between devices  9.53 us (13%)
  starting transfers between devices  7.33 us (10%)
  other arithmetic  6.97 us (9%)
  loops' own time  5.25 us (7%)
    all_to_all x1, blocking collectives, per_device(): got = lax.all_to_all(back, AXES, split_axis=0, concat_axis=0, tiled=True)  13.7 us
    all_to_all x1, waiting for transfers between devices, per_device(): got = lax.all_to_all(payload, AXES, split_axis=0, concat_axis=0, tiled=True)  9.53 us
    all_to_all x1, starting transfers between devices, per_device(): got = lax.all_to_all(payload, AXES, split_axis=0, concat_axis=0, tiled=True)  7.33 us
    concatenate x6, local copies, waits for them, and re-layouts, per_device(): payload = jnp.concatenate([right, obs_weight, kappa_sq[None]], axis=0)  4.47 us
    another operation x1, local copies, waits for them, and re-layouts, per_device(): sums = jnp.stack([jnp.sum(x * y) for x, y in pairs])  3.88 us
    dynamic_update_slice x224, other arithmetic, hour_factors(): return lax.scan(advance, jnp.zeros_like(off), main)[1]  2.81 us
    all_to_all x1, local copies, waits for them, and re-layouts, per_device(): got = lax.all_to_all(payload, AXES, split_axis=0, concat_axis=0, tiled=True)  2.55 us
    another operation x3, loops' own time, hour_solve(): return lax.scan(up, zero, (forward, ratio), reverse=True)[1]  2.27 us
  transfers between devices with their start and end apart: 1, of which 1 were waited for; matrix products, arithmetic and copies ran while one was open for 0% of the time, Pallas kernels for 0%

profile of v1, /device:TPU:0, one launch (start us, length us, event | category | flops | bytes accessed | tf_op | source)
XLA Modules:
  0.0 74.9 jit_solution(9444945120121701400)
XLA Ops:
  0.6 0.8 %sqrt.3 = f32[8,1024]{1,0:T(8,128)S(1)} sqrt(f32[8,1024]{1,0:T(8,128)} %param.25) | non-fusion elementwise | bytes 65536 | tf_op jit(solution)/shard_map/sqrt | solution.py:75
  1.4 1.0 %multiply_add_fusion.2 = (f32[2,8,1024]{2,1,0:T(8,128)S(1)}, f32[2,8,1024]{2,1,0:T(8,128)S(1)}) fusion(f32[2,8,1024]{2,1,0:T(8,128)} %param.22, f32[2,8,1024]{2,1,0:T(8,128)} %param.21, f32[2,8,1024]{2,1,0:T(8,128)} %param.20, s32[2,8,1024]{2,1,0:T(8,128)} %param.23, f32[8,1024]{1,0:T(8,128)S(1)} %sqrt.3, f32[8,1024]{1,0:T(8,128)} %param.25), kind=kLoop, calls=%fused_computation.71 | loop fusion | flops 114688 | bytes 458752 | tf_op jit(solution)/shard_map/add | solution.py:75
  2.4 0.8 %concatenate.20 = f32[2,8,32,32]{3,2,1,0:T(8,128)} reshape(f32[2,8,1024]{2,1,0:T(8,128)S(1)} %get-tuple-element.723) | data formatting | bytes 131072 | tf_op jit(solution)/shard_map/concatenate | solution.py:77
  3.2 0.8 %concatenate.21 = f32[2,8,32,32]{3,2,1,0:T(8,128)} reshape(f32[2,8,1024]{2,1,0:T(8,128)S(1)} %get-tuple-element.724) | data formatting | bytes 131072 | tf_op jit(solution)/shard_map/concatenate | solution.py:77
  4.0 1.5 %concatenate.22 = f32[1,8,32,32]{3,2,1,0:T(8,128)} reshape(f32[8,1024]{1,0:T(8,128)} %param.24) | data formatting | bytes 65536 | tf_op jit(solution)/shard_map/concatenate | solution.py:77
  8.6 1.1 %copy.41 = f32[2,8,32,32]{3,1,0,2:T(8,128)S(1)} copy(f32[2,8,32,32]{3,2,1,0:T(8,128)} %concatenate.20) | data formatting | bytes 131072 | tf_op jit(solution)/shard_map/concatenate | solution.py:77
  10.1 1.8 %concatenate.24 = f32[5,8,32,36]{3,1,0,2:T(8,128)} concatenate(f32[5,8,32,1]{3,1,0,2:T(8,128)S(1)} %copy.61, f32[5,8,32,1]{3,1,0,2:T(8,128)S(1)} %copy.62, f32[5,8,32,32]{3,1,0,2:T(8,128)S(1)} %pad_maximum_fusion, f32[5,8,32,1]{3,1,0,2:T(8,128)S(1)} %copy.63, f32[5,8,32,1]{3,1,0,2:T(8,128)S(1)} %copy.64), dimensions={3} | concatenate | bytes 368640 | tf_op jit(solution)/shard_map/concatenate | solution.py:22
  11.8 2.6 %all_to_all.19 = f32[32,1,1440]{2,1,0:T(1,128)} reshape(f32[32,5,8,36]{3,2,1,0:T(8,128)} %bitcast.136) | data formatting | bytes 368640 | tf_op jit(solution)/shard_map/all_to_all | solution.py:80
  14.4 7.3 %all-to-all-start = ((f32[32,1,1440]{2,1,0:T(1,128)}), f32[32,1,1440]{2,1,0:T(1,128)S(1)}, u32[]{:S(2)}, u32[]{:S(2)}) async-start(f32[32,1,1440]{2,1,0:T(1,128)} %all_to_all.19), calls=%async_computation | async-start | bytes 393216 | tf_op jit(solution)/shard_map/all_to_all | solution.py:80
  21.8 9.5 %all-to-all-done = f32[32,1,1440]{2,1,0:T(1,128)S(1)} async-done(((f32[32,1,1440]{2,1,0:T(1,128)}), f32[32,1,1440]{2,1,0:T(1,128)S(1)}, u32[]{:S(2)}, u32[]{:S(2)}) %all-to-all-start) | async-done | bytes 184352 | tf_op jit(solution)/shard_map/all_to_all | solution.py:80
  32.3 1.1 %while.105 = (s32[]{:T(128)}, f32[16,36]{1,0:T(8,128)S(1)}, f32[32,16,36]{2,1,0:T(8,128)S(1)}, f32[32,16,36]{2,1,0:T(8,128)S(1)}, f32[16,36]{1,0:T(8,128)S(1)}, /*index=5*/s32[]{:T(128)}, s32[]{:T(128)}) while((s32[]{:T(128)}, f32[16,36]{1,0:T(8,128)S(1)}, f32[32,16,36]{2,1,0:T(8,128)S(1)}, f32[32,16,36]{2,1,0:T(8,128)S(1)}, ...), condition=%wide.region_1.2_spmd.clone, body=%wide.region_0.1_spmd.clone.sunk | while | flops 2307 | bytes 41051 | solution.py:30
  33.6 1.2 %while.106 = (s32[]{:T(128)}, f32[16,36]{1,0:T(8,128)S(1)}, f32[32,16,36]{2,1,0:T(8,128)S(1)}, f32[32,16,36]{2,1,0:T(8,128)S(1)}, f32[32,16,36]{2,1,0:T(8,128)S(...) while((s32[]{:T(128)}, f32[16,36]{1,0:T(8,128)S(1)}, f32[32,16,36]{2,1,0:T(8,128)S(1)}, ...), condition=%wide.region_3.4_spmd.clone, body=%wide.region_2.3_spmd.clone.sunk | while | flops 2307 | bytes 49251 | solution.py:45
  34.8 1.1 %while.107 = (s32[]{:T(128)}, f32[16,36]{1,0:T(8,128)S(1)}, f32[32,16,36]{2,1,0:T(8,128)S(1)}, f32[32,16,36]{2,1,0:T(8,128)S(1)}, f32[32,16,36]{2,1,0:T(8,128)S(1)}, /*index=5*/s32[]{:T(128)}, s32[]{:T(128)}, s32[]{:T(128)}) while((s32[]{:T(128)}, f32[16,36]{1,0:T(8,128)S(1)}, f32[32,16,36]{2,1,0:T(8,128)S(1)}, ...), condition=%wide.region_5.6_spmd.clone, body=%wide.region_4.5_spmd.clone.sunk | while | flops 1732 | bytes 41071 | solution.py:46
  36.3 1.2 %while.108 = (s32[]{:T(128)}, f32[16,36]{1,0:T(8,128)S(1)}, f32[32,16,36]{2,1,0:T(8,128)S(1)}, f32[32,16,36]{2,1,0:T(8,128)S(1)}, f32[32,16,36]{2,1,0:T(8,128)S(...) while((s32[]{:T(128)}, f32[16,36]{1,0:T(8,128)S(1)}, f32[32,16,36]{2,1,0:T(8,128)S(1)}, ...), condition=%wide.region_7.8_spmd.clone, body=%wide.region_6.7_spmd.clone.sunk | while | flops 2307 | bytes 49251 | solution.py:45
  37.5 1.1 %while.109 = (s32[]{:T(128)}, f32[16,36]{1,0:T(8,128)S(1)}, f32[32,16,36]{2,1,0:T(8,128)S(1)}, f32[32,16,36]{2,1,0:T(8,128)S(1)}, f32[32,16,36]{2,1,0:T(8,128)S(1)}, /*index=5*/s32[]{:T(128)}, s32[]{:T(128)}, s32[]{:T(128)}) while((s32[]{:T(128)}, f32[16,36]{1,0:T(8,128)S(1)}, f32[32,16,36]{2,1,0:T(8,128)S(1)}, ...), condition=%wide.region_9.10_spmd.clone, body=%wide.region_8.9_spmd.clone.sunk | while | flops 1732 | bytes 41071 | solution.py:46
  38.9 1.1 %multiply_reduce_fusion = (f32[]{:T(128)}, f32[]{:T(128)}, f32[]{:T(128)}, f32[]{:T(128)}, f32[]{:T(128)}, /*index=5*/f32[]{:T(128)}, f32[32,16,32]{2,1,0:T(8,12...) fusion(f32[32,16,36]{2,1,0:T(8,128)S(1)} %fusion.14, ...), kind=kLoop, calls=%fused_computation.57 | loop fusion | flops 196602 | bytes 589848 | tf_op jit(solution)/shard_map/reduce_sum | solution.py:105
  40.1 1.2 %while.110 = (s32[]{:T(128)}, f32[16,36]{1,0:T(8,128)S(1)}, f32[32,16,36]{2,1,0:T(8,128)S(1)}, f32[32,16,36]{2,1,0:T(8,128)S(1)}, f32[32,16,36]{2,1,0:T(8,128)S(...) while((s32[]{:T(128)}, f32[16,36]{1,0:T(8,128)S(1)}, f32[32,16,36]{2,1,0:T(8,128)S(1)}, ...), condition=%wide.region_11.12_spmd.clone, body=%wide.region_10.11_spmd.clone.sunk | while | flops 2307 | bytes 49251 | solution.py:45
  41.3 1.1 %while.111 = (s32[]{:T(128)}, f32[16,36]{1,0:T(8,128)S(1)}, f32[32,16,36]{2,1,0:T(8,128)S(1)}, f32[32,16,36]{2,1,0:T(8,128)S(1)}, f32[32,16,36]{2,1,0:T(8,128)S(1)}, /*index=5*/s32[]{:T(128)}, s32[]{:T(128)}, s32[]{:T(128)}) while((s32[]{:T(128)}, f32[16,36]{1,0:T(8,128)S(1)}, f32[32,16,36]{2,1,0:T(8,128)S(1)}, ...), condition=%wide.region_13.14_spmd.clone, body=%wide.region_12.13_spmd.clone.sunk | while | flops 1732 | bytes 41071 | solution.py:46
  43.3 3.9 %stack.51 = f32[6]{0:T(128)S(1)} concatenate(f32[1]{0:T(128)} %bitcast.12, f32[1]{0:T(128)} %bitcast.13, f32[1]{0:T(128)} %bitcast.14, f32[1]{0:T(128)} %bitcast.15, f32[1]{0:T(128)} %bitcast.16, f32[1]{0:T(128)} %bitcast.17), dimensions={0} | concatenate | bytes 48 | tf_op jit(solution)/shard_map/stack | solution.py:105
  47.6 13.7 %all_to_all.22 = f32[32,1,2566]{2,1,0:T(1,128)S(1)} all-to-all(f32[32,1,2566]{2,1,0:T(1,128)S(1)} %copy.54), channel_id=1, replica_groups=mesh['tm'=16,'rows'=2] {'tm','rows'}, dimensions={0} | all-to-all | bytes 656896 | tf_op jit(solution)/shard_map/all_to_all | solution.py:110
  61.3 0.7 fusion.32
  72.6 0.8 %add.210 = f32[2,8,1024]{2,1,0:T(8,128)} reshape(f32[1,2,8,32,32]{4,3,2,1,0:T(8,128)S(1)} %copy.55) | data formatting | bytes 131072 | tf_op jit(solution)/shard_map/add | solution.py:116
  73.5 0.8 %add.215 = f32[2,8,1024]{2,1,0:T(8,128)} reshape(f32[1,2,8,32,32]{4,3,2,1,0:T(8,128)S(1)} %copy.58) | data formatting | bytes 131072 | tf_op jit(solution)/shard_map/add | solution.py:118
  74.3 0.6 add_add_fusion
  (296 shorter events, 10.3 us)
Async XLA Ops:
  0.6 4.9 %copy-start.2 = (f32[8,1024]{1,0:T(8,128)S(1)}, f32[8,1024]{1,0:T(8,128)}, u32[]{:S(2)}) copy-start(f32[8,1024]{1,0:T(8,128)} %param.24) | copy-start | bytes 98308
  8.2 1.5 %copy-start = (f32[2,8,32,32]{3,2,1,0:T(8,128)S(1)}, f32[2,8,32,32]{3,2,1,0:T(8,128)}, u32[]{:S(2)}) copy-start(f32[2,8,32,32]{3,2,1,0:T(8,128)} %concatenate.21) | copy-start | bytes 196612
  8.2 1.7 %copy-start.1 = (f32[1,8,32,32]{3,2,1,0:T(8,128)S(1)}, f32[1,8,32,32]{3,2,1,0:T(8,128)}, u32[]{:S(2)}) copy-start(f32[1,8,32,32]{3,2,1,0:T(8,128)} %concatenate.22) | copy-start | bytes 98308
  14.4 17.0 %all-to-all-start = ((f32[32,1,1440]{2,1,0:T(1,128)}), f32[32,1,1440]{2,1,0:T(1,128)S(1)}, u32[]{:S(2)}, u32[]{:S(2)}) async-start(f32[32,1,1440]{2,1,0:T(1,128)} %all_to_all.19), calls=%async_computation | async-start | bytes 393216 | tf_op jit(solution)/shard_map/all_to_all | solution.py:80

commit v2 on v1

--- a/solution.py
+++ b/solution.py
@@ -1,6 +1,8 @@
 import jax
 import jax.numpy as jnp
 from jax import lax
+from jax.experimental import pallas as pl
+from jax.experimental.pallas import tpu as pltpu
 from jax.sharding import PartitionSpec as P
 
 ITERS = 2
@@ -63,7 +65,7 @@
     return alpha + beta * g, beta * alpha, delta - beta * g, alpha + beta * g - beta * alpha
 
 
-def per_device(observations, obs_noise, prior_noise, observed, kappa_sq, obs_precision):
+def per_device_any(observations, obs_noise, prior_noise, observed, kappa_sq, obs_precision):
     hours, rows, columns = observations.shape
     over_tm, over_rows = lax.axis_size("tm"), lax.axis_size("rows")
     blocks = over_tm * over_rows
@@ -119,6 +121,270 @@
     )
 
 
+LANES, SUB = 128, 8
+HALF = LANES // 2
+PAD = 4
+
+
+def lanes_of():
+    lane = lax.broadcasted_iota(jnp.int32, (SUB, LANES), 1)
+    sub = lax.broadcasted_iota(jnp.int32, (SUB, LANES), 0)
+    return lane, sub
+
+
+def turn(x, shift):
+    shift = shift % LANES
+    return x if shift == 0 else pltpu.roll(x, shift, 1)
+
+
+def pack_kernel(blocks, obs, noise, prior, observed, kappa, precision, right, out, weight):
+    hours, _, columns = obs.shape
+    width = columns // blocks
+    lane, _ = lanes_of()
+    prec = precision[...]
+    root = jnp.sqrt(prec)
+    for h in range(hours):
+        mask = observed[h].astype(jnp.float32)
+        right[h] = mask * (prec * obs[h] + root * noise[h]) + prior[h]
+        weight[h] = mask * prec
+    zero = jnp.zeros((SUB, LANES), jnp.float32)
+
+    def tile(ref, k):
+        inside = 0 <= k < columns // LANES
+        return ref[:, k * LANES : (k + 1) * LANES] if inside else zero
+
+    def window(ref, block):
+        k, at = divmod(block * width, LANES)
+        here = tile(ref, k)
+        if at < ITERS:
+            here = jnp.where(lane >= HALF, tile(ref, k - 1), here)
+        if at + width + ITERS > LANES:
+            here = jnp.where(lane < HALF, tile(ref, k + 1), here)
+        return here, at
+
+    low = lax.rem(lane + PAD, LANES) < HALF
+    spot = width + ITERS + PAD
+    piece = width // 2 + ITERS
+    third = (lane >= spot - 1) & (lane < HALF - PAD)
+    for block in range(blocks):
+        kap, at = window(kappa, block)
+        for h in range(hours):
+            lo = turn(window(right.at[h], block)[0], -at)
+            hi = turn(window(weight.at[h], block)[0], HALF - at)
+            chunk = jnp.where(low, lo, hi)
+            if h < 2:
+                chunk = jnp.where(third, turn(kap, spot - (at - ITERS + h * piece)), chunk)
+            out[block, h] = chunk
+
+
+def solve_kernel(columns, got, out, right, inv, rat, z0, y1, y2, s1, s2):
+    blocks, hb = got.shape[:2]
+    strips = 2
+    every = blocks // strips * hb
+    width = columns // blocks
+    half = every // 2
+    lane, sub = lanes_of()
+    low = lax.rem(lane + PAD, LANES) < HALF
+    place = lax.rem(lane + PAD, HALF) - PAD
+    block = lax.axis_index("tm") * strips + lax.axis_index("rows")
+    column = block * width + place
+    inside = (place >= -ITERS) & (place < width + ITERS) & (column >= 0) & (column < columns)
+    own = (place >= 0) & (place < width)
+    spot = width + ITERS + PAD
+    piece = width // 2 + ITERS
+
+    def pieces(h):
+        return jnp.where(low, got[0, h], turn(got[1, h], HALF))
+
+    kap = jnp.where(
+        place < piece - ITERS, turn(pieces(0), -ITERS - spot), turn(pieces(1), piece - ITERS - spot)
+    )
+    window = (place >= -ITERS) & (place < width + ITERS)
+    diag = jnp.where(window, kap, 0.0) + 4.0
+    off = -coupling * diag
+    off_sq = off * off
+    inner = (1.0 + coupling * coupling) * diag
+    zero = jnp.zeros((SUB, LANES), jnp.float32)
+
+    def hour_weight(t):
+        return 1.0 if t in (0, every - 1) else 1.0 + coupling * coupling
+
+    order = [(i, every - 1 - i) for i in range(half)]
+    before = [None, None]
+    for both in order:
+        for side, t in enumerate(both):
+            src, h = divmod(t, hb)
+            c0, c1 = got[strips * src, h], got[strips * src + 1, h]
+            rhs = jnp.where(low, c0, turn(c1, HALF))
+            main = jnp.where(low, turn(c0, HALF), c1) + (
+                diag if t in (0, every - 1) else inner
+            )
+            pivot = main if before[side] is None else main - off_sq * before[side][0]
+            iv = 1.0 / pivot
+            c = off * iv
+            g = rhs * iv if before[side] is None else rhs * iv - c * before[side][1]
+            right[t], inv[t], rat[t], z0[t] = rhs, iv, c, g
+            before[side] = (iv, g)
+    top, low_t = half - 1, half
+    joint = 1.0 / (1.0 - rat[top] * rat[low_t])
+
+    def outward(ref):
+        c_top, c_low = rat[top], rat[low_t]
+        a = (ref[top] - c_top * ref[low_t]) * joint
+        b = ref[low_t] - c_low * a
+        ref[top], ref[low_t] = a, b
+        for i in range(1, half):
+            a = ref[top - i] - rat[top - i] * a
+            b = ref[low_t + i] - rat[low_t + i] * b
+            ref[top - i], ref[low_t + i] = a, b
+
+    def inward(source, ref):
+        a = b = None
+        for i, j in order:
+            a = source[i] * inv[i] if a is None else source[i] * inv[i] - rat[i] * a
+            b = source[j] * inv[j] if b is None else source[j] * inv[j] - rat[j] * b
+            ref[i], ref[j] = a, b
+
+    last, initial = sub == SUB - 1, sub == 0
+    edge = (last & ~low) | (initial & low)
+
+    def beside(v):
+        across = jnp.where(edge, turn(v, HALF), 0.0)
+        up = pltpu.roll(jnp.where(last, across, v), 1, 0)
+        down = pltpu.roll(jnp.where(initial, across, v), SUB - 1, 0)
+        return (up + down) + (turn(v, 1) + turn(v, -1))
+
+    def split(ref, result):
+        old, now = zero, beside(ref[0])
+        for t in range(every):
+            new = beside(ref[t + 1]) if t + 1 < every else zero
+            value = hour_weight(t) * now - coupling * (old + new)
+            result[t] = jnp.where(inside, value, 0.0)
+            old, now = now, new
+
+    outward(z0)
+    split(z0, s1)
+    inward(s1, y1)
+    outward(y1)
+    split(y1, s2)
+    inward(s2, y2)
+    outward(y2)
+
+    total = zero
+    pairs = ((right, z0), (z0, s1), (right, y1), (s1, y1), (z0, s2), (y1, s2))
+    for row, (x, y) in enumerate(pairs):
+        parts = [x[t] * y[t] for t in range(4)]
+        for t in range(4, every):
+            parts[t % 4] = parts[t % 4] + x[t] * y[t]
+        part = jnp.where(own, (parts[0] + parts[1]) + (parts[2] + parts[3]), 0.0)
+        part = jnp.sum(part, axis=0, keepdims=True)
+        total = jnp.where(sub == row, part, total)
+    total = total + turn(total, HALF)
+
+    first = lax.rem(lane, HALF) < HALF // 2
+    left = lane < HALF
+
+    def two(a, b):
+        return jnp.where(first, a, turn(b, HALF // 2))
+
+    total = two(total, zero)
+    for src in range(blocks // strips):
+        t = src * hb
+        groups = (
+            (two(z0[t], z0[t + 1]), two(s1[t], s1[t + 1])),
+            (two(y1[t], y1[t + 1]), two(s2[t], s2[t + 1])),
+            (two(y2[t], y2[t + 1]), total),
+        )
+        for g, (a, b) in enumerate(groups):
+            out[strips * src, g] = jnp.where(left, a, turn(b, HALF))
+            out[strips * src + 1, g] = jnp.where(left, turn(a, HALF), b)
+
+
+def unpack_kernel(got, right, solution, residual, precond):
+    blocks = got.shape[0]
+    lane, _ = lanes_of()
+    left = lane < HALF
+    first = lax.rem(lane, HALF) < HALF // 2
+    parts = [got[c, 2] for c in range(4)]
+    for c in range(4, blocks):
+        parts[c % 4] = parts[c % 4] + got[c, 2]
+    total = (parts[0] + parts[1]) + (parts[2] + parts[3])
+    total = jnp.sum(jnp.where(left, 0.0, total), axis=1, keepdims=True)
+    total = jnp.broadcast_to(total, (SUB, LANES))
+    sums = [jnp.broadcast_to(total[i : i + 1], (SUB, LANES)) for i in range(6)]
+    cx, c2, c0, c1 = step_scalars(*sums)
+    k0, k1, k2 = jnp.where(left, c0, c1), jnp.where(left, c1, c2), jnp.where(left, c2, 0.0)
+    per = 4
+    for tile in range(blocks // per):
+        at = pl.ds(tile * LANES, LANES)
+        mixed, iterate = [], []
+        for c in range(tile * per, tile * per + per):
+            v0, v1, v2 = got[c, 0], got[c, 1], got[c, 2]
+            mixed.append(k0 * v0 + k1 * v1 + k2 * v2)
+            iterate.append(cx * v0 + c2 * v1)
+
+        def heads(q):
+            return [jnp.where(left, q[i], turn(q[i + 2], HALF)) for i in (0, 1)]
+
+        def tails(q):
+            return [jnp.where(left, turn(q[i], HALF), q[i + 2]) for i in (0, 1)]
+
+        def spread(p):
+            step = HALF // 2
+            return (
+                jnp.where(first, p[0], turn(p[1], step)),
+                jnp.where(first, turn(p[0], -step), p[1]),
+            )
+
+        for h, value in enumerate(spread(heads(iterate))):
+            solution[h, :, at] = value
+        for h, value in enumerate(spread(heads(mixed))):
+            precond[h, :, at] = value
+        for h, value in enumerate(spread(tails(mixed))):
+            residual[h, :, at] = c0 * right[h, :, at] + value
+
+
+def per_device(observations, obs_noise, prior_noise, observed, kappa_sq, obs_precision):
+    hours, rows, columns = observations.shape
+    blocks = lax.axis_size("tm") * lax.axis_size("rows")
+    fits = (
+        lax.axis_size("rows") == 2
+        and hours == 2
+        and rows == SUB
+        and columns % LANES == 0
+        and columns == blocks * (LANES // 4)
+    )
+    args = (observations, obs_noise, prior_noise, observed, kappa_sq, obs_precision)
+    if not fits:
+        return per_device_any(*args)
+    every = blocks // 2 * hours
+
+    def shaped(*shape):
+        return jax.ShapeDtypeStruct(shape, jnp.float32)
+
+    right, chunks = pl.pallas_call(
+        lambda *refs: pack_kernel(blocks, *refs),
+        out_shape=(shaped(hours, rows, columns), shaped(blocks, hours, rows, LANES)),
+        scratch_shapes=[pltpu.VMEM((hours, rows, columns), jnp.float32)],
+        name="pack",
+    )(*args)
+    got = lax.all_to_all(chunks, AXES, split_axis=0, concat_axis=0, tiled=True)
+    chunks = pl.pallas_call(
+        lambda *refs: solve_kernel(columns, *refs),
+        out_shape=shaped(blocks, 3, rows, LANES),
+        scratch_shapes=[pltpu.VMEM((every, rows, LANES), jnp.float32)] * 8,
+        name="solve",
+    )(got)
+    got = lax.all_to_all(chunks, AXES, split_axis=0, concat_axis=0, tiled=True)
+    return tuple(
+        pl.pallas_call(
+            unpack_kernel,
+            out_shape=[shaped(hours, rows, columns)] * 3,
+            name="unpack",
+        )(got, right)
+    )
+
+
 def solution(mesh):
     whole, plane = P("tm", "rows", None), P("rows", None)
     return jax.shard_map(

time: 75.5 us -> 42 us (0.56)
  local copies, waits for them, and re-layouts: 21.4 us -> 0 us
  blocking collectives: 13.7 us -> 34.1 us
  between operations: 10.7 us -> 0.63 us
  waiting for transfers between devices: 9.53 us -> 0 us
  starting transfers between devices: 7.33 us -> 0 us
  other arithmetic: 6.97 us -> 0 us
  Pallas kernels: 0 us -> 6.68 us
  loops' own time: 5.25 us -> 0 us
    all_to_all x1 -> x2, blocking collectives: 13.7 us -> 34.1 us  [per_device(): got = lax.all_to_all(chunks, AXES, split_axis=0, concat_axis=0, tiled=True)]
    all_to_all x1 -> x0, waiting for transfers between devices: 9.53 us -> none  [per_device(): got = lax.all_to_all(payload, AXES, split_axis=0, concat_axis=0, tiled=True)]
    all_to_all x1 -> x0, starting transfers between devices: 7.33 us -> none  [per_device(): got = lax.all_to_all(payload, AXES, split_axis=0, concat_axis=0, tiled=True)]
    pallas_call x0 -> x3, Pallas kernels: none -> 6.68 us  [the longest x1 2.87 us: per_device(): pl.pallas_call(lambda *refs: solve_kernel(columns, *refs), out_shape=shap...]
    concatenate x8 -> x0, local copies, waits for them, and re-layouts: 6.26 us -> none  [the longest x6 4.47 us: per_device(): payload = jnp.concatenate([right, obs_weight, kappa_sq[None]], axis=0)]
    another operation x7 -> x0, loops' own time: 5.25 us -> none  [the longest x3 2.27 us: hour_solve(): return lax.scan(up, zero, (forward, ratio), reverse=True)[1]]
    another operation x11 -> x0, local copies, waits for them, and re-layouts: 4.78 us -> none  [the longest x1 3.88 us: per_device(): sums = jnp.stack([jnp.sum(x * y) for x, y in pairs])]
    all_to_all x2 -> x0, local copies, waits for them, and re-layouts: 2.91 us -> none  [the longest x1 2.55 us: per_device(): got = lax.all_to_all(payload, AXES, split_axis=0, concat_axis=0, tiled=True)]
  transfers between devices with their start and end apart: 1 -> 0, of which waited for: 1 -> 0; matrix products, arithmetic and copies ran while one was open for 0% -> 0% of each run, Pallas kernels for 0% -> 0%
where the time goes in v2:
time: 42 us; the launch traced here: 41.4 us
  blocking collectives  34.1 us (81%)
  Pallas kernels  6.68 us (16%)
  between operations  0.63 us (2%)
    all_to_all x2, blocking collectives, per_device(): got = lax.all_to_all(chunks, AXES, split_axis=0, concat_axis=0, tiled=True)  34.1 us
    pallas_call x1, Pallas kernels, per_device(): pl.pallas_call(lambda *refs: solve_kernel(columns, *refs), out_shape=shap...  2.87 us
    pallas_call x1, Pallas kernels, per_device(): pl.pallas_call(unpack_kernel, out_shape=[shaped(hours, rows, columns)] *...  1.94 us
    pallas_call x1, Pallas kernels, per_device(): pl.pallas_call(lambda *refs: pack_kernel(blocks, *refs), out_shape=(shape...  1.87 us

profile of v2, /device:TPU:0, one launch (start us, length us, event | category | flops | bytes accessed | tf_op | source)
XLA Modules:
  0.0 41.4 jit_solution(17862217699264202608)
XLA Ops:
  0.6 1.9 %pack.1 = (f32[2,8,1024]{2,1,0:T(8,128)}, f32[32,2,8,128]{3,2,1,0:T(8,128)}) custom-call(f32[2,8,1024]{2,1,0:T(8,128)} %refs_0_.1, f32[2,8,1024]{2,1,0:T(8,128)} %refs_1_.1, f32[2,8,1024]{2,1,0:T(8,128)} %refs_2_.1, s32[2,8,1024]{2,1,0:T(8,128)} %refs_3_.1, f32[8,1024]{1,0:T(8,128)} %refs_4_.1, f32[8,1024]{1,0:T(8,128)} %refs_5_.1), custom_call_target="tpu_custom_call" | custom-call | tf_op jit(solution)/shard_map/pack/pallas_call | solution.py:365
  2.5 18.1 %all_to_all.10.refs_0_ = f32[32,2,8,128]{3,2,1,0:T(8,128)} all-to-all(f32[32,2,8,128]{3,2,1,0:T(8,128)} %get-tuple-element.5), channel_id=1, replica_groups=mesh['tm'=16,'rows'=2] {'tm','rows'}, dimensions={0} | all-to-all | bytes 524288 | tf_op jit(solution)/shard_map/all_to_all | solution.py:371
  20.6 2.9 %solve.1 = f32[32,3,8,128]{3,2,1,0:T(8,128)} custom-call(f32[32,2,8,128]{3,2,1,0:T(8,128)} %all_to_all.10.refs_0_), custom_call_target="tpu_custom_call" | custom-call | tf_op jit(solution)/shard_map/solve/pallas_call | solution.py:372
  23.5 16.0 %all_to_all.11.got = f32[32,3,8,128]{3,2,1,0:T(8,128)} all-to-all(f32[32,3,8,128]{3,2,1,0:T(8,128)} %solve.1), channel_id=1, replica_groups=mesh['tm'=16,'rows'=2] {'tm','rows'}, dimensions={0} | all-to-all | bytes 786432 | tf_op jit(solution)/shard_map/all_to_all | solution.py:378
  39.5 1.9 %unpack.1 = (f32[2,8,1024]{2,1,0:T(8,128)}, f32[2,8,1024]{2,1,0:T(8,128)}, f32[2,8,1024]{2,1,0:T(8,128)}) custom-call(f32[32,3,8,128]{3,2,1,0:T(8,128)} %all_to_all.11.got, f32[2,8,1024]{2,1,0:T(8,128)} %get-tuple-element.6.right), custom_call_target="tpu_custom_call" | custom-call | tf_op jit(solution)/shard_map/unpack/pallas_call | solution.py:380

commit v3 on v1

--- a/solution.py
+++ b/solution.py
@@ -1,6 +1,8 @@
 import jax
 import jax.numpy as jnp
 from jax import lax
+from jax.experimental import pallas as pl
+from jax.experimental.pallas import tpu as pltpu
 from jax.sharding import PartitionSpec as P
 
 ITERS = 2
@@ -63,7 +65,7 @@
     return alpha + beta * g, beta * alpha, delta - beta * g, alpha + beta * g - beta * alpha
 
 
-def per_device(observations, obs_noise, prior_noise, observed, kappa_sq, obs_precision):
+def per_device_any(observations, obs_noise, prior_noise, observed, kappa_sq, obs_precision):
     hours, rows, columns = observations.shape
     over_tm, over_rows = lax.axis_size("tm"), lax.axis_size("rows")
     blocks = over_tm * over_rows
@@ -119,6 +121,399 @@
     )
 
 
+LANES, SUB = 128, 8
+HALF = LANES // 2
+SLOTS = 4
+SLOT = LANES // SLOTS
+EXTRA = 2
+
+
+def lanes_of():
+    lane = lax.broadcasted_iota(jnp.int32, (SUB, LANES), 1)
+    sub = lax.broadcasted_iota(jnp.int32, (SUB, LANES), 0)
+    return lane, sub
+
+
+def turn(x, shift):
+    shift = shift % LANES
+    return x if shift == 0 else pltpu.roll(x, shift, 1)
+
+
+def halves(a, b, left):
+    return jnp.where(left, a, turn(b, HALF)), jnp.where(left, turn(a, HALF), b)
+
+
+def quad(q, left, first):
+    p0, p2 = halves(q[0], q[2], left)
+    p1, p3 = halves(q[1], q[3], left)
+    result = []
+    for a, b in ((p0, p1), (p2, p3)):
+        result.append(jnp.where(first, a, turn(b, SLOT)))
+        result.append(jnp.where(first, turn(a, -SLOT), b))
+    return result
+
+
+def tile(ref, k, *row):
+    at = pl.ds(k * LANES, LANES)
+    return ref[row + (slice(None), at)] if row else ref[:, at]
+
+
+def pack_kernel(obs, noise, prior, observed, kappa, precision, right, weight, out):
+    hours, _, columns = obs.shape
+    tiles = columns // LANES
+    blocks = tiles * SLOTS
+    lane, sub = lanes_of()
+    left = lane < HALF
+    slot_lane = lax.rem(lane, SLOT)
+    first = lax.rem(lane, HALF) < SLOT
+    rows = SUB + EXTRA
+    prec = precision[...]
+    root = jnp.sqrt(prec)
+    for h in range(hours):
+        mask = observed[h].astype(jnp.float32)
+        right[h] = mask * (prec * obs[h] + root * noise[h]) + prior[h]
+        weight[h] = mask * prec
+    zero = jnp.zeros((SUB, LANES), jnp.float32)
+
+    span = 2 * ITERS
+    beginnings, endings = [], []
+    for k in range(tiles):
+        items = [tile(ref, k, h) for ref in (right, weight) for h in range(hours)]
+        for j, chunk in enumerate(quad(items, left, first)):
+            out[pl.ds((k * SLOTS + j) * rows, SUB), :] = chunk
+        begin, end = zero, zero
+        for i, item in enumerate(items):
+            at = i * span
+            begin = jnp.where(slot_lane // ITERS == i * 2 + 1, turn(item, at + ITERS), begin)
+            end = jnp.where(slot_lane // ITERS == i * 2, turn(item, at - SLOT + ITERS), end)
+        falling = lax.rem(SUB - sub, SUB)
+        beginnings.append(jnp.take_along_axis(begin, falling, axis=0))
+        endings.append(jnp.take_along_axis(end, falling, axis=0))
+
+    line = lax.rem(lax.axis_index("tm"), SUB)
+    kap = [
+        jnp.sum(jnp.where(sub == line, tile(kappa, k), 0.0), axis=0, keepdims=True)
+        for k in range(tiles)
+    ]
+    wide = len(items) * span
+    before = lax.rem(lane // ITERS, 2) == 0
+    lane_row = lax.broadcasted_iota(jnp.int32, (1, LANES), 1)
+    for block in range(blocks):
+        k, j = divmod(block, SLOTS)
+        at = j * SLOT
+        prev = turn(endings[(block - 1) // SLOTS], SLOT - at) if block else zero
+        last = block == blocks - 1
+        follow = zero if last else turn(beginnings[(block + 1) // SLOTS], -at - SLOT)
+        halo = jnp.where(lane < wide, jnp.where(before, prev, follow), 0.0)
+        halo = pltpu.roll(halo, 0, 1, stride=wide, stride_axis=0)
+        out[pl.ds(block * rows + SUB, 1), :] = jnp.sum(halo, axis=0, keepdims=True)
+        here = kap[k]
+        if j == 0 and k > 0:
+            here = jnp.where(lane_row >= HALF, kap[k - 1], here)
+        if j == SLOTS - 1 and k + 1 < tiles:
+            here = jnp.where(lane_row < HALF, kap[k + 1], here)
+        out[pl.ds(block * rows + SUB + 1, 1), :] = turn(here, -at)
+
+
+def solve_kernel(columns, got, out, right, inv, rat, z0, y1, y2, s1, s2, side):
+    strips, hb = 2, 2
+    rows = SUB + EXTRA
+    blocks = got.shape[0] // rows
+    pairs = blocks // strips
+    every = pairs * hb
+    width = SLOT
+    half = every // 2
+    lane, sub = lanes_of()
+    left = lane < HALF
+    first = lax.rem(lane, HALF) < SLOT
+    low = lax.rem(lane + ITERS, LANES) < HALF
+    place = lax.rem(lane + ITERS, HALF) - ITERS
+    block = lax.axis_index("tm") * strips + lax.axis_index("rows")
+    column = block * width + place
+    window = place < width + ITERS
+    inside = window & (column >= 0) & (column < columns)
+    own = (place >= 0) & (place < width)
+    ahead = place < 0
+    zero = jnp.zeros((SUB, LANES), jnp.float32)
+
+    def strip_rows(at):
+        return [jnp.broadcast_to(got[pl.ds(at + s * rows, 1), :], (SUB, LANES)) for s in (0, 1)]
+
+    kap = [zero, zero]
+    for i in range(SUB):
+        lines = strip_rows(i * strips * rows + SUB + 1)
+        kap = [jnp.where(sub == i, line, k) for line, k in zip(lines, kap)]
+    kap = jnp.where(low, kap[0], turn(kap[1], HALF))
+    diag = jnp.where(window, kap, 0.0) + 4.0
+    off = -coupling * diag
+    off_sq = off * off
+    inner = (1.0 + coupling * coupling) * diag
+
+    span = 2 * ITERS
+    wide = 2 * hb * span
+
+    def fields(pair):
+        at = pair * strips * rows
+        c0, c1 = got[pl.ds(at, SUB), :], got[pl.ds(at + rows, SUB), :]
+        h0, h1 = (
+            pltpu.roll(line, 0, 1, stride=wide, stride_axis=0)
+            for line in strip_rows(at + SUB)
+        )
+        halo = jnp.where(left, h0, turn(h1, HALF))
+        result = []
+        for i, mine in enumerate(halves(c0, c1, left)):
+            for h in range(hb):
+                item = i * hb + h
+                around = jnp.where(
+                    ahead,
+                    turn(halo, -ITERS - item * span),
+                    turn(halo, SLOT - ITERS - item * span),
+                )
+                result.append(jnp.where(own, turn(mine, -h * SLOT), around))
+        return result
+
+    def hour_weight(t):
+        return 1.0 if t in (0, every - 1) else 1.0 + coupling * coupling
+
+    def eliminate(t, rhs, weight, before):
+        main = jnp.where(window, weight, 0.0) + (diag if t in (0, every - 1) else inner)
+        pivot = main if before is None else main - off_sq * before[0]
+        iv = 1.0 / pivot
+        c = off * iv
+        g = rhs * iv if before is None else rhs * iv - c * before[1]
+        right[t], inv[t], rat[t], z0[t] = rhs, iv, c, g
+        return iv, g
+
+    upper = lower = None
+    for i in range(0, half, hb):
+        r_a, r_b, w_a, w_b = fields(i // hb)
+        q_a, q_b, v_a, v_b = fields(pairs - 1 - i // hb)
+        upper = eliminate(i, r_a, w_a, upper)
+        lower = eliminate(every - 1 - i, q_b, v_b, lower)
+        upper = eliminate(i + 1, r_b, w_b, upper)
+        lower = eliminate(every - 2 - i, q_a, v_a, lower)
+    top, low_t = half - 1, half
+    joint = 1.0 / (1.0 - rat[top] * rat[low_t])
+
+    def outward(ref):
+        a = (ref[top] - rat[top] * ref[low_t]) * joint
+        b = ref[low_t] - rat[low_t] * a
+        ref[top], ref[low_t] = a, b
+        for i in range(1, half):
+            a = ref[top - i] - rat[top - i] * a
+            b = ref[low_t + i] - rat[low_t + i] * b
+            ref[top - i], ref[low_t + i] = a, b
+
+    def inward(source, ref):
+        a = b = None
+        for i in range(half):
+            j = every - 1 - i
+            a = source[i] * inv[i] if a is None else source[i] * inv[i] - rat[i] * a
+            b = source[j] * inv[j] if b is None else source[j] * inv[j] - rat[j] * b
+            ref[i], ref[j] = a, b
+
+    last, initial = sub == SUB - 1, sub == 0
+    edge = (last & ~low) | (initial & low)
+    low_row = low[:1]
+
+    def beside(v, t, base):
+        across = jnp.where(edge, turn(v, HALF), 0.0)
+        line = jnp.where(low_row, across[:1], across[SUB - 1 :])
+        pair, h = divmod(t, hb)
+        side[pair, base + 1 + h : base + 2 + h] = line
+        other, spot = (pair - 1, hb + 1) if h == 0 else (pair + 1, 0)
+        if 0 <= other < pairs:
+            side[other, base + spot : base + spot + 1] = line
+        up = pltpu.roll(jnp.where(last, across, v), 1, 0)
+        down = pltpu.roll(jnp.where(initial, across, v), SUB - 1, 0)
+        return (up + down) + (turn(v, 1) + turn(v, -1))
+
+    def split(ref, result, base):
+        old, now = zero, beside(ref[0], 0, base)
+        for t in range(every):
+            new = beside(ref[t + 1], t + 1, base) if t + 1 < every else zero
+            value = hour_weight(t) * now - coupling * (old + new)
+            result[t] = jnp.where(inside, value, 0.0)
+            old, now = now, new
+
+    side[0], side[pairs - 1] = zero, zero
+    outward(z0)
+    split(z0, s1, 0)
+    inward(s1, y1)
+    outward(y1)
+    split(y1, s2, hb + 2)
+    inward(s2, y2)
+    outward(y2)
+
+    total = zero
+    products = ((right, z0), (z0, s1), (right, y1), (s1, y1), (z0, s2), (y1, s2))
+    for row, (x, y) in enumerate(products):
+        parts = [x[t] * y[t] for t in range(4)]
+        for t in range(4, every):
+            parts[t % 4] = parts[t % 4] + x[t] * y[t]
+        part = jnp.where(own, (parts[0] + parts[1]) + (parts[2] + parts[3]), 0.0)
+        part = jnp.sum(part, axis=0, keepdims=True)
+        total = jnp.where(sub == row, part, total)
+    total = turn(total + turn(total, HALF), SLOT)
+
+    def two(ref, pair):
+        before = ref[pair * hb - 1] if pair > 0 else zero
+        after = ref[pair * hb + hb] if pair + 1 < pairs else zero
+        return jnp.where(first, before, turn(after, SLOT))
+
+    for pair in range(pairs):
+        groups = (
+            (two(z0, pair), two(y1, pair)),
+            (two(y2, pair), jnp.where(first, side[pair], total)),
+        )
+        for g, (a, b) in enumerate(groups):
+            for strip, chunk in enumerate(halves(a, b, left)):
+                out[strips * pair + strip, g] = chunk
+
+
+def unpack_kernel(got, right, weight, kappa, solution, residual, precond, z0, y1, y2, side):
+    blocks = got.shape[0]
+    tiles = blocks // SLOTS
+    hb = 2
+    lane, sub = lanes_of()
+    left = lane < HALF
+    first = lax.rem(lane, HALF) < SLOT
+    parts = [got[c, 1] for c in range(4)]
+    for c in range(4, blocks):
+        parts[c % 4] = parts[c % 4] + got[c, 1]
+    total = (parts[0] + parts[1]) + (parts[2] + parts[3])
+    total = jnp.sum(jnp.where(lane >= LANES - SLOT, total, 0.0), axis=1, keepdims=True)
+    total = jnp.broadcast_to(total, (SUB, LANES))
+    sums = [jnp.broadcast_to(total[i : i + 1], (SUB, LANES)) for i in range(6)]
+    cx, c2, c0, c1 = step_scalars(*sums)
+
+    for k in range(tiles):
+        at = pl.ds(k * LANES, LANES)
+        early, late = (
+            quad([got[k * SLOTS + j, g] for j in range(SLOTS)], left, first) for g in (0, 1)
+        )
+        z0[0, :, at], z0[hb + 1, :, at] = early[0], early[1]
+        y1[0, :, at], y1[hb + 1, :, at] = early[2], early[3]
+        y2[0, :, at], y2[1, :, at] = late[0], late[1]
+        side[:, at] = late[2]
+
+    mine, strip = lax.axis_index("tm"), lax.axis_index("rows")
+    inner = 1.0 + coupling * coupling
+    e_a = jnp.where(mine == 0, 1.0, inner)
+    e_b = jnp.where(mine == lax.axis_size("tm") - 1, 1.0, inner)
+    last, initial = sub == SUB - 1, sub == 0
+    edge = (sub == jnp.where(strip == 0, 0, SUB - 1))
+
+    def block_solve(k, f_a, f_b, before, after):
+        diag = tile(kappa, k) + 4.0
+        off = -coupling * diag
+        d_a = e_a * diag + tile(weight, k, 0)
+        d_b = e_b * diag + tile(weight, k, 1)
+        scale = 1.0 / (d_a * d_b - off * off)
+        f_a, f_b = f_a - off * before, f_b - off * after
+        return (d_b * f_a - off * f_b) * scale, (d_a * f_b - off * f_a) * scale
+
+    def split(ref, base):
+        forward = [[turn(tile(ref, k, q), 1) for k in range(tiles)] for q in range(hb + 2)]
+        back = [[turn(tile(ref, k, q), -1) for k in range(tiles)] for q in range(hb + 2)]
+        result = []
+        for k in range(tiles):
+            near = []
+            for q in range(hb + 2):
+                v = tile(ref, k, q)
+                line = side[base + q : base + q + 1, pl.ds(k * LANES, LANES)]
+                across = jnp.where(edge, line, 0.0)
+                up = pltpu.roll(jnp.where(last, across, v), 1, 0)
+                down = pltpu.roll(jnp.where(initial, across, v), SUB - 1, 0)
+                west = jnp.where(lane == 0, forward[q][k - 1] if k else 0.0, forward[q][k])
+                east = back[q][k + 1] if k + 1 < tiles else 0.0
+                east = jnp.where(lane == LANES - 1, east, back[q][k])
+                near.append((up + down) + (east + west))
+            result.append(
+                (
+                    e_a * near[1] - coupling * (near[0] + near[2]),
+                    e_b * near[2] - coupling * (near[1] + near[3]),
+                )
+            )
+        return result
+
+    for k in range(tiles):
+        at = pl.ds(k * LANES, LANES)
+        z0[1, :, at], z0[2, :, at] = block_solve(
+            k, tile(right, k, 0), tile(right, k, 1), tile(z0, k, 0), tile(z0, k, 3)
+        )
+    s1 = split(z0, 0)
+    for k in range(tiles):
+        at = pl.ds(k * LANES, LANES)
+        pair = block_solve(k, *s1[k], tile(y1, k, 0), tile(y1, k, 3))
+        for h in range(hb):
+            y1[h + 1, :, at] = pair[h]
+            solution[h, :, at] = cx * tile(z0, k, h + 1) + c2 * pair[h]
+            residual[h, :, at] = c0 * tile(right, k, h) + c1 * s1[k][h]
+    s2 = split(y1, hb + 2)
+    for k in range(tiles):
+        at = pl.ds(k * LANES, LANES)
+        pair = block_solve(k, *s2[k], tile(y2, k, 0), tile(y2, k, 1))
+        for h in range(hb):
+            residual[h, :, at] = tile(residual, k, h) + c2 * s2[k][h]
+            precond[h, :, at] = (
+                c0 * tile(z0, k, h + 1) + c1 * tile(y1, k, h + 1) + c2 * pair[h]
+            )
+
+
+def exchange(chunks, blocks):
+    rows = chunks.shape[0] // blocks
+    chunks = chunks.reshape(blocks, rows // EXTRA, EXTRA, LANES)
+    return lax.all_to_all(chunks, AXES, split_axis=0, concat_axis=0, tiled=True).reshape(-1, LANES)
+
+
+def per_device(observations, obs_noise, prior_noise, observed, kappa_sq, obs_precision):
+    hours, rows, columns = observations.shape
+    pairs = lax.axis_size("tm")
+    blocks = pairs * lax.axis_size("rows")
+    fits = (
+        lax.axis_size("rows") == 2
+        and hours == 2
+        and rows == SUB
+        and columns == blocks * SLOT
+        and pairs >= SUB
+        and pairs % 2 == 0
+    )
+    args = (observations, obs_noise, prior_noise, observed, kappa_sq, obs_precision)
+    if not fits:
+        return per_device_any(*args)
+
+    def shaped(*shape):
+        return jax.ShapeDtypeStruct(shape, jnp.float32)
+
+    def room(*shape):
+        return pltpu.VMEM(shape, jnp.float32)
+
+    field = shaped(hours, rows, columns)
+    right, weight, chunks = pl.pallas_call(
+        pack_kernel,
+        out_shape=(field, field, shaped(blocks * (rows + EXTRA), LANES)),
+        name="pack",
+    )(*args)
+    got = exchange(chunks, blocks)
+    chunks = pl.pallas_call(
+        lambda *refs: solve_kernel(columns, *refs),
+        out_shape=shaped(blocks, 2, rows, LANES),
+        scratch_shapes=[room(pairs * hours, rows, LANES)] * 8 + [room(pairs, rows, LANES)],
+        name="solve",
+    )(got)
+    got = lax.all_to_all(chunks, AXES, split_axis=0, concat_axis=0, tiled=True)
+    return tuple(
+        pl.pallas_call(
+            unpack_kernel,
+            out_shape=[field] * 3,
+            scratch_shapes=[room(hours + 2, rows, columns)] * 2
+            + [room(2, rows, columns), room(rows, columns)],
+            name="unpack",
+        )(got, right, weight, kappa_sq)
+    )
+
+
 def solution(mesh):
     whole, plane = P("tm", "rows", None), P("rows", None)
     return jax.shard_map(

time: 75.5 us -> 39.2 us (0.52)
  local copies, waits for them, and re-layouts: 21.4 us -> 0 us
  blocking collectives: 13.7 us -> 30.5 us
  between operations: 10.7 us -> 0.63 us
  waiting for transfers between devices: 9.53 us -> 0 us
  Pallas kernels: 0 us -> 7.73 us
  starting transfers between devices: 7.33 us -> 0 us
  other arithmetic: 6.97 us -> 0 us
  loops' own time: 5.25 us -> 0 us
    all_to_all x1 -> x2, blocking collectives: 13.7 us -> 30.5 us  [the longest x1 16.6 us: exchange(): lax.all_to_all(chunks, AXES, split_axis=0, concat_axis=0, tiled=True)]
    all_to_all x1 -> x0, waiting for transfers between devices: 9.53 us -> none  [per_device(): got = lax.all_to_all(payload, AXES, split_axis=0, concat_axis=0, tiled=True)]
    pallas_call x0 -> x3, Pallas kernels: none -> 7.73 us  [the longest x1 2.87 us: per_device(): pl.pallas_call(lambda *refs: solve_kernel(columns, *refs), out_shape=shap...]
    all_to_all x1 -> x0, starting transfers between devices: 7.33 us -> none  [per_device(): got = lax.all_to_all(payload, AXES, split_axis=0, concat_axis=0, tiled=True)]
    concatenate x8 -> x0, local copies, waits for them, and re-layouts: 6.26 us -> none  [the longest x6 4.47 us: per_device(): payload = jnp.concatenate([right, obs_weight, kappa_sq[None]], axis=0)]
    another operation x7 -> x0, loops' own time: 5.25 us -> none  [the longest x3 2.27 us: hour_solve(): return lax.scan(up, zero, (forward, ratio), reverse=True)[1]]
    another operation x11 -> x0, local copies, waits for them, and re-layouts: 4.78 us -> none  [the longest x1 3.88 us: per_device(): sums = jnp.stack([jnp.sum(x * y) for x, y in pairs])]
    all_to_all x2 -> x0, local copies, waits for them, and re-layouts: 2.91 us -> none  [the longest x1 2.55 us: per_device(): got = lax.all_to_all(payload, AXES, split_axis=0, concat_axis=0, tiled=True)]
  transfers between devices with their start and end apart: 1 -> 0, of which waited for: 1 -> 0; matrix products, arithmetic and copies ran while one was open for 0% -> 0% of each run, Pallas kernels for 0% -> 0%
where the time goes in v3:
time: 39.2 us; the launch traced here: 38.9 us
  blocking collectives  30.5 us (78%)
  Pallas kernels  7.73 us (20%)
  between operations  0.63 us (2%)
    all_to_all x1, blocking collectives, exchange(): lax.all_to_all(chunks, AXES, split_axis=0, concat_axis=0, tiled=True)  16.6 us
    all_to_all x1, blocking collectives, per_device(): got = lax.all_to_all(chunks, AXES, split_axis=0, concat_axis=0, tiled=True)  13.9 us
    pallas_call x1, Pallas kernels, per_device(): pl.pallas_call(lambda *refs: solve_kernel(columns, *refs), out_shape=shap...  2.87 us
    pallas_call x1, Pallas kernels, per_device(): pl.pallas_call(unpack_kernel, out_shape=[field] * 3, scratch_shapes=[room...  2.59 us
    pallas_call x1, Pallas kernels, per_device(): pl.pallas_call(pack_kernel, out_shape=(field, field, shaped(blocks * (row...  2.27 us

profile of v3, /device:TPU:0, one launch (start us, length us, event | category | flops | bytes accessed | tf_op | source)
XLA Modules:
  0.0 38.9 jit_solution(14671810300257299671)
XLA Ops:
  0.6 2.3 %pack.1 = (f32[2,8,1024]{2,1,0:T(8,128)}, f32[2,8,1024]{2,1,0:T(8,128)}, f32[320,128]{1,0:T(8,128)}) custom-call(f32[2,8,1024]{2,1,0:T(8,128)} %obs.1, f32[2,8,1024]{2,1,0:T(8,128)} %noise.1, f32[2,8,1024]{2,1,0:T(8,128)} %prior.1, s32[2,8,1024]{2,1,0:T(8,128)} %observed.1, f32[8,1024]{1,0:T(8,128)} %kappa.3, f32[8,1024]{1,0:T(8,128)} %precision.1), custom_call_target="tpu_custom_call" | custom-call | tf_op jit(solution)/shard_map/pack/pallas_call | solution.py:493
  2.9 16.6 %all_to_all.10 = f32[32,5,2,128]{3,2,1,0:T(2,128)} all-to-all(f32[32,5,2,128]{3,2,1,0:T(2,128)} %bitcast.3), channel_id=1, replica_groups=mesh['tm'=16,'rows'=2] {'tm','rows'}, dimensions={0} | all-to-all | bytes 327680 | tf_op jit(solution)/shard_map/all_to_all | solution.py:467
  19.5 2.9 %solve.1 = f32[32,2,8,128]{3,2,1,0:T(8,128)} custom-call(f32[320,128]{1,0:T(8,128)} %bitcast.2), custom_call_target="tpu_custom_call" | custom-call | tf_op jit(solution)/shard_map/solve/pallas_call | solution.py:499
  22.3 13.9 %all_to_all.11.got = f32[32,2,8,128]{3,2,1,0:T(8,128)} all-to-all(f32[32,2,8,128]{3,2,1,0:T(8,128)} %solve.1), channel_id=1, replica_groups=mesh['tm'=16,'rows'=2] {'tm','rows'}, dimensions={0} | all-to-all | bytes 524288 | tf_op jit(solution)/shard_map/all_to_all | solution.py:505
  36.3 2.6 %unpack.1 = (f32[2,8,1024]{2,1,0:T(8,128)}, f32[2,8,1024]{2,1,0:T(8,128)}, f32[2,8,1024]{2,1,0:T(8,128)}) custom-call(f32[32,2,8,128]{3,2,1,0:T(8,128)} %all_to_all.11.got, f32[2,8,1024]{2,1,0:T(8,128)} %get-tuple-element.7.right, f32[2,8,1024]{2,1,0:T(8,128)} %get-tuple-element.8.weight, f32[8,1024]{1,0:T(8,128)} %kappa.3), custom_call_target="tpu_custom_call" | custom-call | tf_op jit(solution)/shard_map/unpack/pallas_call | solution.py:507

commit v4 on v3

--- a/solution.py
+++ b/solution.py
@@ -492,16 +492,20 @@
     field = shaped(hours, rows, columns)
     right, weight, chunks = pl.pallas_call(
         pack_kernel,
-        out_shape=(field, field, shaped(blocks * (rows + EXTRA), LANES)),
+        out_shape=(
+            pltpu.VMEM((hours, rows, columns), jnp.float32),
+            pltpu.VMEM((hours, rows, columns), jnp.float32),
+            pltpu.VMEM((blocks * (rows + EXTRA), LANES), jnp.float32),
+        ),
         name="pack",
     )(*args)
     got = exchange(chunks, blocks)
     chunks = pl.pallas_call(
         lambda *refs: solve_kernel(columns, *refs),
-        out_shape=shaped(blocks, 2, rows, LANES),
+        out_shape=pltpu.VMEM((blocks, 2, rows, LANES), jnp.float32),
         scratch_shapes=[room(pairs * hours, rows, LANES)] * 8 + [room(pairs, rows, LANES)],
         name="solve",
-    )(got)
+    )(pltpu.with_memory_space_constraint(got, pltpu.VMEM))
     got = lax.all_to_all(chunks, AXES, split_axis=0, concat_axis=0, tiled=True)
     return tuple(
         pl.pallas_call(
@@ -510,7 +514,7 @@
             scratch_shapes=[room(hours + 2, rows, columns)] * 2
             + [room(2, rows, columns), room(rows, columns)],
             name="unpack",
-        )(got, right, weight, kappa_sq)
+        )(*(pltpu.with_memory_space_constraint(x, pltpu.VMEM) for x in (got, right, weight, kappa_sq)))
     )
 
 

time: 39.2 us -> 34.1 us (0.87)
  Pallas kernels: 7.73 us -> 4.53 us
  blocking collectives: 30.5 us -> 28.6 us
    pallas_call x2, Pallas kernels: 5.15 us -> 2.88 us  [the longest x1 1.61 us: per_device(): pl.pallas_call(pack_kernel, out_shape=(pltpu.VMEM((hours, rows, columns),...]
    all_to_all x1, blocking collectives: 13.9 us -> 12.4 us  [per_device(): got = lax.all_to_all(chunks, AXES, split_axis=0, concat_axis=0, tiled=True)]
    pallas_call x1, Pallas kernels: 2.59 us -> 1.66 us  [per_device(): pl.pallas_call(unpack_kernel, out_shape=[field] * 3, scratch_shapes=[room...]
where the time goes in v4:
time: 34.1 us; the launch traced here: 33.8 us
  blocking collectives  28.6 us (84%)
  Pallas kernels  4.53 us (13%)
  between operations  0.65 us (2%)
    all_to_all x1, blocking collectives, exchange(): lax.all_to_all(chunks, AXES, split_axis=0, concat_axis=0, tiled=True)  16.2 us
    all_to_all x1, blocking collectives, per_device(): got = lax.all_to_all(chunks, AXES, split_axis=0, concat_axis=0, tiled=True)  12.4 us
    pallas_call x1, Pallas kernels, per_device(): pl.pallas_call(unpack_kernel, out_shape=[field] * 3, scratch_shapes=[room...  1.66 us
    pallas_call x1, Pallas kernels, per_device(): pl.pallas_call(pack_kernel, out_shape=(pltpu.VMEM((hours, rows, columns),...  1.61 us
    pallas_call x1, Pallas kernels, per_device(): pl.pallas_call(lambda *refs: solve_kernel(columns, *refs), out_shape=pltp...  1.27 us

profile of v4, /device:TPU:0, one launch (start us, length us, event | category | flops | bytes accessed | tf_op | source)
XLA Modules:
  0.0 33.8 jit_solution(6339716831184006709)
XLA Ops:
  0.6 1.6 %pack.1 = (f32[2,8,1024]{2,1,0:T(8,128)S(1)}, f32[2,8,1024]{2,1,0:T(8,128)S(1)}, f32[320,128]{1,0:T(8,128)S(1)}) custom-call(f32[2,8,1024]{2,1,0:T(8,128)} %obs.1, f32[2,8,1024]{2,1,0:T(8,128)} %noise.1, f32[2,8,1024]{2,1,0:T(8,128)} %prior.1, s32[2,8,1024]{2,1,0:T(8,128)} %observed.1, f32[8,1024]{1,0:T(8,128)} %kappa.3, f32[8,1024]{1,0:T(8,128)} %precision.1), custom_call_target="tpu_custom_call" | custom-call | tf_op jit(solution)/shard_map/pack/pallas_call | solution.py:493
  2.2 16.2 %all_to_all.10 = f32[32,5,2,128]{3,2,1,0:T(2,128)S(1)} all-to-all(f32[32,5,2,128]{3,2,1,0:T(2,128)S(1)} %bitcast.3), channel_id=1, replica_groups=mesh['tm'=16,'rows'=2] {'tm','rows'}, dimensions={0} | all-to-all | bytes 327680 | tf_op jit(solution)/shard_map/all_to_all | solution.py:467
  18.5 1.3 %solve.1 = f32[32,2,8,128]{3,2,1,0:T(8,128)S(1)} custom-call(f32[320,128]{1,0:T(8,128)S(1)} %bitcast.2), custom_call_target="tpu_custom_call" | custom-call | tf_op jit(solution)/shard_map/solve/pallas_call | solution.py:503
  19.8 0.0 copy-start
  19.8 12.4 %all_to_all.11.got = f32[32,2,8,128]{3,2,1,0:T(8,128)S(1)} all-to-all(f32[32,2,8,128]{3,2,1,0:T(8,128)S(1)} %solve.1), channel_id=1, replica_groups=mesh['tm'=16,'rows'=2] {'tm','rows'}, dimensions={0} | all-to-all | bytes 524288 | tf_op jit(solution)/shard_map/all_to_all | solution.py:509
  32.2 0.0 copy-done
  32.2 1.7 %unpack.1 = (f32[2,8,1024]{2,1,0:T(8,128)}, f32[2,8,1024]{2,1,0:T(8,128)}, f32[2,8,1024]{2,1,0:T(8,128)}) custom-call(f32[32,2,8,128]{3,2,1,0:T(8,128)S(1)} %all_to_all.11.got, f32[2,8,1024]{2,1,0:T(8,128)S(1)} %get-tuple-element.7.right, f32[2,8,1024]{2,1,0:T(8,128)S(1)} %get-tuple-element.8.weight, f32[8,1024]{1,0:T(8,128)S(1)} %copy-done), custom_call_target="tpu_custom_call" | custom-call | tf_op jit(solution)/shard_map/unpack/pallas_call | solution.py:511
Async XLA Ops:
  19.8 12.4 %copy-start = (f32[8,1024]{1,0:T(8,128)S(1)}, f32[8,1024]{1,0:T(8,128)}, u32[]{:S(2)}) copy-start(f32[8,1024]{1,0:T(8,128)} %kappa.3) | copy-start | bytes 98308

commit v5 on v4

--- a/solution.py
+++ b/solution.py
@@ -176,7 +176,9 @@
     zero = jnp.zeros((SUB, LANES), jnp.float32)
 
     span = 2 * ITERS
-    beginnings, endings = [], []
+    wide = 2 * hours * span
+    before = lax.rem(lane // ITERS, 2) == 0
+    ends, begins = [], []
     for k in range(tiles):
         items = [tile(ref, k, h) for ref in (right, weight) for h in range(hours)]
         for j, chunk in enumerate(quad(items, left, first)):
@@ -186,33 +188,54 @@
             at = i * span
             begin = jnp.where(slot_lane // ITERS == i * 2 + 1, turn(item, at + ITERS), begin)
             end = jnp.where(slot_lane // ITERS == i * 2, turn(item, at - SLOT + ITERS), end)
-        falling = lax.rem(SUB - sub, SUB)
-        beginnings.append(jnp.take_along_axis(begin, falling, axis=0))
-        endings.append(jnp.take_along_axis(end, falling, axis=0))
+        ends.append(turn(end, SLOT))
+        begins.append(turn(begin, -SLOT))
+
+    def before_tile(k):
+        return jnp.where(lane < SLOT, ends[k - 1] if k else 0.0, ends[k])
+
+    def after_tile(k):
+        return jnp.where(
+            lane >= LANES - SLOT, begins[k + 1] if k + 1 < tiles else 0.0, begins[k]
+        )
 
     line = lax.rem(lax.axis_index("tm"), SUB)
     kap = [
-        jnp.sum(jnp.where(sub == line, tile(kappa, k), 0.0), axis=0, keepdims=True)
+        jnp.broadcast_to(
+            jnp.sum(jnp.where(sub == line, tile(kappa, k), 0.0), axis=0, keepdims=True),
+            (SUB, LANES),
+        )
         for k in range(tiles)
     ]
-    wide = len(items) * span
-    before = lax.rem(lane // ITERS, 2) == 0
-    lane_row = lax.broadcasted_iota(jnp.int32, (1, LANES), 1)
-    for block in range(blocks):
-        k, j = divmod(block, SLOTS)
-        at = j * SLOT
-        prev = turn(endings[(block - 1) // SLOTS], SLOT - at) if block else zero
-        last = block == blocks - 1
-        follow = zero if last else turn(beginnings[(block + 1) // SLOTS], -at - SLOT)
-        halo = jnp.where(lane < wide, jnp.where(before, prev, follow), 0.0)
+
+    def kappa_rows(k):
+        here = jnp.where((sub < 2) & (lane >= HALF), kap[max(k - 1, 0)], kap[k])
+        return jnp.where(
+            (sub // 2 == 1) & (lane < HALF), kap[min(k + 1, tiles - 1)], here
+        )
+
+    falling = lax.rem(SUB - sub, SUB)
+    swapped = lax.rem(lane // wide + sub, SUB)
+    for k in range(0, tiles, 2):
+        near = [
+            jnp.where(slot_lane < wide, of(k), turn(of(k + 1), wide))
+            for of in (before_tile, after_tile)
+        ]
+        halo = jnp.where(before, near[0], pltpu.roll(near[1], SUB - 2, 0))
+        halo = jnp.take_along_axis(halo, falling, axis=0)
         halo = pltpu.roll(halo, 0, 1, stride=wide, stride_axis=0)
-        out[pl.ds(block * rows + SUB, 1), :] = jnp.sum(halo, axis=0, keepdims=True)
-        here = kap[k]
-        if j == 0 and k > 0:
-            here = jnp.where(lane_row >= HALF, kap[k - 1], here)
-        if j == SLOTS - 1 and k + 1 < tiles:
-            here = jnp.where(lane_row < HALF, kap[k + 1], here)
-        out[pl.ds(block * rows + SUB + 1, 1), :] = turn(here, -at)
+        halo = jnp.take_along_axis(halo, swapped, axis=0)
+        halo = pltpu.roll(halo, 0, 1, stride=wide, stride_axis=0)
+        lines = jnp.where(
+            lax.rem(sub, 2) == 0, kappa_rows(k), turn(kappa_rows(k + 1), -SLOT // 2)
+        )
+        lines = pltpu.roll(lines, 0, 1, stride=SLOT // 2, stride_axis=0)
+        for r in range(SUB):
+            group = (SUB - r) % SUB
+            block = (k + group % 2) * SLOTS + group // 2
+            out[pl.ds(block * rows + SUB, 1), :] = halo[r : r + 1]
+            block = (k + r % 2) * SLOTS + (SLOTS - r // 2) % SLOTS
+            out[pl.ds(block * rows + SUB + 1, 1), :] = lines[r : r + 1]
 
 
 def solve_kernel(columns, got, out, right, inv, rat, z0, y1, y2, s1, s2, side):
@@ -233,7 +256,6 @@
     window = place < width + ITERS
     inside = window & (column >= 0) & (column < columns)
     own = (place >= 0) & (place < width)
-    ahead = place < 0
     zero = jnp.zeros((SUB, LANES), jnp.float32)
 
     def strip_rows(at):
@@ -264,34 +286,34 @@
         for i, mine in enumerate(halves(c0, c1, left)):
             for h in range(hb):
                 item = i * hb + h
-                around = jnp.where(
-                    ahead,
-                    turn(halo, -ITERS - item * span),
-                    turn(halo, SLOT - ITERS - item * span),
-                )
+                around = turn(halo, -ITERS - item * span)
                 result.append(jnp.where(own, turn(mine, -h * SLOT), around))
         return result
 
     def hour_weight(t):
         return 1.0 if t in (0, every - 1) else 1.0 + coupling * coupling
 
-    def eliminate(t, rhs, weight, before):
-        main = jnp.where(window, weight, 0.0) + (diag if t in (0, every - 1) else inner)
-        pivot = main if before is None else main - off_sq * before[0]
-        iv = 1.0 / pivot
-        c = off * iv
-        g = rhs * iv if before is None else rhs * iv - c * before[1]
-        right[t], inv[t], rat[t], z0[t] = rhs, iv, c, g
-        return iv, g
+    def main_of(t, weight):
+        return jnp.where(window, weight, 0.0) + (diag if t in (0, every - 1) else inner)
+
+    def eliminate(hours, rhs, weights, before):
+        main = [main_of(t, w) for t, w in zip(hours, weights)]
+        pivot = main[0] if before is None else main[0] - off_sq * before[0]
+        inv_a = 1.0 / pivot
+        inv_b = pivot * (1.0 / (pivot * main[1] - off_sq))
+        g = None if before is None else before[1]
+        for t, r, iv in zip(hours, rhs, (inv_a, inv_b)):
+            c = off * iv
+            g = r * iv if g is None else r * iv - c * g
+            right[t], inv[t], rat[t], z0[t] = r, iv, c, g
+        return inv_b, g
 
     upper = lower = None
     for i in range(0, half, hb):
         r_a, r_b, w_a, w_b = fields(i // hb)
         q_a, q_b, v_a, v_b = fields(pairs - 1 - i // hb)
-        upper = eliminate(i, r_a, w_a, upper)
-        lower = eliminate(every - 1 - i, q_b, v_b, lower)
-        upper = eliminate(i + 1, r_b, w_b, upper)
-        lower = eliminate(every - 2 - i, q_a, v_a, lower)
+        upper = eliminate((i, i + 1), (r_a, r_b), (w_a, w_b), upper)
+        lower = eliminate((every - 1 - i, every - 2 - i), (q_b, q_a), (v_b, v_a), lower)
     top, low_t = half - 1, half
     joint = 1.0 / (1.0 - rat[top] * rat[low_t])
 
@@ -345,119 +367,168 @@
     inward(s2, y2)
     outward(y2)
 
-    total = zero
+    totals = [zero, zero]
     products = ((right, z0), (z0, s1), (right, y1), (s1, y1), (z0, s2), (y1, s2))
-    for row, (x, y) in enumerate(products):
+    for i, (x, y) in enumerate(products):
         parts = [x[t] * y[t] for t in range(4)]
         for t in range(4, every):
             parts[t % 4] = parts[t % 4] + x[t] * y[t]
         part = jnp.where(own, (parts[0] + parts[1]) + (parts[2] + parts[3]), 0.0)
         part = jnp.sum(part, axis=0, keepdims=True)
-        total = jnp.where(sub == row, part, total)
-    total = turn(total + turn(total, HALF), SLOT)
+        totals[i // 3] = jnp.where(sub == i % 3 + 2, part, totals[i // 3])
+    totals = [part + turn(part, HALF) for part in totals]
+    totals = [part + turn(part, -SLOT // 2) for part in totals]
+    low_part = lax.rem(lane, SLOT) < SLOT // 2
+    total = jnp.where(low_part, turn(totals[0], SLOT), turn(totals[1], SLOT + SLOT // 2))
 
     def two(ref, pair):
         before = ref[pair * hb - 1] if pair > 0 else zero
         after = ref[pair * hb + hb] if pair + 1 < pairs else zero
         return jnp.where(first, before, turn(after, SLOT))
 
+    size = out.shape[0] // blocks
+    inner_w = 1.0 + coupling * coupling
+    hour_row = lax.rem(sub, hb + 2)
+
+    def edge_rows(pair):
+        lines = side[pair]
+        weight = inner_w
+        if pair == 0:
+            weight = jnp.where(hour_row == 0, 1.0, inner_w)
+        if pair == pairs - 1:
+            weight = jnp.where(hour_row == 1, 1.0, inner_w)
+        around = lines + pltpu.roll(lines, SUB - 2, 0)
+        added = weight * pltpu.roll(lines, SUB - 1, 0) - coupling * around
+        return jnp.where(sub < 4, pltpu.roll(added, 2, 0), added)
+
     for pair in range(pairs):
-        groups = (
-            (two(z0, pair), two(y1, pair)),
-            (two(y2, pair), jnp.where(first, side[pair], total)),
-        )
-        for g, (a, b) in enumerate(groups):
-            for strip, chunk in enumerate(halves(a, b, left)):
-                out[strips * pair + strip, g] = chunk
-
-
-def unpack_kernel(got, right, weight, kappa, solution, residual, precond, z0, y1, y2, side):
-    blocks = got.shape[0]
+        mine = two(y2, pair)
+        other = jnp.where(first, edge_rows(pair), total)
+        other = jnp.where(sub >= SUB - 2, mine, other)
+        for strip, chunk in enumerate(halves(pltpu.roll(mine, 2, 0), other, left)):
+            out[pl.ds((strips * pair + strip) * size + SUB - 2, SUB), :] = chunk
+        for strip, chunk in enumerate(halves(two(z0, pair), two(y1, pair), left)):
+            out[pl.ds((strips * pair + strip) * size, SUB), :] = chunk
+
+
+def at_hour(t, rows=SUB, shift=0):
+    return pl.ds((t + 1) * SUB + shift, rows)
+
+
+def unpack_kernel(
+    got, right, weight, kappa, solution, residual, precond, z0, y1, y2, side, coef
+):
+    hb = 2
+    size = 2 * SUB - 2
+    blocks = got.shape[0] // size
     tiles = blocks // SLOTS
-    hb = 2
     lane, sub = lanes_of()
     left = lane < HALF
     first = lax.rem(lane, HALF) < SLOT
-    parts = [got[c, 1] for c in range(4)]
-    for c in range(4, blocks):
-        parts[c % 4] = parts[c % 4] + got[c, 1]
-    total = (parts[0] + parts[1]) + (parts[2] + parts[3])
-    total = jnp.sum(jnp.where(lane >= LANES - SLOT, total, 0.0), axis=1, keepdims=True)
-    total = jnp.broadcast_to(total, (SUB, LANES))
-    sums = [jnp.broadcast_to(total[i : i + 1], (SUB, LANES)) for i in range(6)]
-    cx, c2, c0, c1 = step_scalars(*sums)
-
-    for k in range(tiles):
-        at = pl.ds(k * LANES, LANES)
-        early, late = (
-            quad([got[k * SLOTS + j, g] for j in range(SLOTS)], left, first) for g in (0, 1)
-        )
-        z0[0, :, at], z0[hb + 1, :, at] = early[0], early[1]
-        y1[0, :, at], y1[hb + 1, :, at] = early[2], early[3]
-        y2[0, :, at], y2[1, :, at] = late[0], late[1]
-        side[:, at] = late[2]
-
     mine, strip = lax.axis_index("tm"), lax.axis_index("rows")
     inner = 1.0 + coupling * coupling
     e_a = jnp.where(mine == 0, 1.0, inner)
     e_b = jnp.where(mine == lax.axis_size("tm") - 1, 1.0, inner)
-    last, initial = sub == SUB - 1, sub == 0
-    edge = (sub == jnp.where(strip == 0, 0, SUB - 1))
-
-    def block_solve(k, f_a, f_b, before, after):
+
+    for k in range(tiles):
         diag = tile(kappa, k) + 4.0
         off = -coupling * diag
         d_a = e_a * diag + tile(weight, k, 0)
         d_b = e_b * diag + tile(weight, k, 1)
         scale = 1.0 / (d_a * d_b - off * off)
-        f_a, f_b = f_a - off * before, f_b - off * after
-        return (d_b * f_a - off * f_b) * scale, (d_a * f_b - off * f_a) * scale
+        coef[0, k], coef[1, k], coef[2, k], coef[3, k] = d_b * scale, off * scale, d_a * scale, off
+
+    def early_of(c):
+        return got[pl.ds(c * size, SUB), :]
+
+    def late_of(c):
+        return got[pl.ds(c * size + SUB - 2, SUB), :]
+
+    def spot(q, k):
+        return q * tiles + k
+
+    parts = [late_of(c) for c in range(4)]
+    for c in range(4, blocks):
+        parts[c % 4] = parts[c % 4] + late_of(c)
+    total = (parts[0] + parts[1]) + (parts[2] + parts[3])
+    sums = []
+    for i in range(2):
+        begin = LANES - SLOT + i * (SLOT // 2)
+        here = (lane >= begin) & (lane < begin + SLOT // 2)
+        part = jnp.sum(jnp.where(here, total, 0.0), axis=1, keepdims=True)
+        part = jnp.broadcast_to(part, (SUB, LANES))
+        sums += [jnp.broadcast_to(part[r : r + 1], (SUB, LANES)) for r in range(2, 5)]
+    cx, c2, c0, c1 = step_scalars(*sums)
+
+    for k in range(tiles):
+        group = range(k * SLOTS, k * SLOTS + SLOTS)
+        early = quad([early_of(c) for c in group], left, first)
+        for ref, b, a in ((z0, early[0], early[1]), (y1, early[2], early[3])):
+            ref[at_hour(spot(0, k)), :], ref[at_hour(spot(hb + 1, k)), :] = b, a
+        q = [late_of(c) for c in group]
+        (p0, p2), (p1, p3) = halves(q[0], q[2], left), halves(q[1], q[3], left)
+        p0, p1 = (
+            jnp.where(sub < SUB - 2, pltpu.roll(p, SUB - 2, 0), high)
+            for p, high in ((p0, p2), (p1, p3))
+        )
+        y2[0, k] = jnp.where(first, p0, turn(p1, SLOT))
+        y2[1, k] = jnp.where(first, turn(p0, -SLOT), p1)
+        side[k] = jnp.where(first, p2, turn(p3, SLOT))
+
+    last, initial = sub == SUB - 1, sub == 0
+    edge = sub == jnp.where(strip == 0, SUB - 1, 0)
+
+    def block_solve(k, f_a, f_b, before, after):
+        f_a, f_b = f_a - coef[3, k] * before, f_b - coef[3, k] * after
+        return coef[0, k] * f_a - coef[1, k] * f_b, coef[2, k] * f_b - coef[1, k] * f_a
+
+    quarter = range(hb + 2)
 
     def split(ref, base):
-        forward = [[turn(tile(ref, k, q), 1) for k in range(tiles)] for q in range(hb + 2)]
-        back = [[turn(tile(ref, k, q), -1) for k in range(tiles)] for q in range(hb + 2)]
-        result = []
+        passed = [0.0] * (hb + 2)
+        back = [turn(ref[at_hour(spot(q, 0)), :], -1) for q in quarter]
         for k in range(tiles):
+            forward = [turn(ref[at_hour(spot(q, k)), :], 1) for q in quarter]
+            more = k + 1 < tiles
+            coming = [
+                turn(ref[at_hour(spot(q, k + 1)), :], -1) if more else 0.0 for q in quarter
+            ]
             near = []
-            for q in range(hb + 2):
-                v = tile(ref, k, q)
-                line = side[base + q : base + q + 1, pl.ds(k * LANES, LANES)]
-                across = jnp.where(edge, line, 0.0)
-                up = pltpu.roll(jnp.where(last, across, v), 1, 0)
-                down = pltpu.roll(jnp.where(initial, across, v), SUB - 1, 0)
-                west = jnp.where(lane == 0, forward[q][k - 1] if k else 0.0, forward[q][k])
-                east = back[q][k + 1] if k + 1 < tiles else 0.0
-                east = jnp.where(lane == LANES - 1, east, back[q][k])
+            for q in quarter:
+                v = ref[at_hour(spot(q, k)), :]
+                up = pltpu.roll(jnp.where(last, 0.0, v), 1, 0)
+                down = pltpu.roll(jnp.where(initial, 0.0, v), SUB - 1, 0)
+                west = jnp.where(lane == 0, passed[q], forward[q])
+                east = jnp.where(lane == LANES - 1, coming[q], back[q])
                 near.append((up + down) + (east + west))
-            result.append(
-                (
-                    e_a * near[1] - coupling * (near[0] + near[2]),
-                    e_b * near[2] - coupling * (near[1] + near[3]),
-                )
-            )
-        return result
+            result = []
+            for h, e in enumerate((e_a, e_b)):
+                line = jnp.where(edge, side[k, base + h : base + h + 1, :], 0.0)
+                result.append(e * near[h + 1] - coupling * (near[h] + near[h + 2]) + line)
+            yield k, *result
+            passed, back = forward, coming
+
+    def hour(ref, q, k):
+        return ref[at_hour(spot(q, k)), :]
 
     for k in range(tiles):
+        z0[at_hour(spot(1, k)), :], z0[at_hour(spot(2, k)), :] = block_solve(
+            k, tile(right, k, 0), tile(right, k, 1), hour(z0, 0, k), hour(z0, 3, k)
+        )
+    for k, *s1 in split(z0, 2):
         at = pl.ds(k * LANES, LANES)
-        z0[1, :, at], z0[2, :, at] = block_solve(
-            k, tile(right, k, 0), tile(right, k, 1), tile(z0, k, 0), tile(z0, k, 3)
-        )
-    s1 = split(z0, 0)
-    for k in range(tiles):
+        pair = block_solve(k, *s1, hour(y1, 0, k), hour(y1, 3, k))
+        for h in range(hb):
+            y1[at_hour(spot(h + 1, k)), :] = pair[h]
+            solution[h, :, at] = cx * hour(z0, h + 1, k) + c2 * pair[h]
+            residual[h, :, at] = c0 * tile(right, k, h) + c1 * s1[h]
+    for k, *s2 in split(y1, 4):
         at = pl.ds(k * LANES, LANES)
-        pair = block_solve(k, *s1[k], tile(y1, k, 0), tile(y1, k, 3))
+        pair = block_solve(k, *s2, y2[0, k], y2[1, k])
         for h in range(hb):
-            y1[h + 1, :, at] = pair[h]
-            solution[h, :, at] = cx * tile(z0, k, h + 1) + c2 * pair[h]
-            residual[h, :, at] = c0 * tile(right, k, h) + c1 * s1[k][h]
-    s2 = split(y1, hb + 2)
-    for k in range(tiles):
-        at = pl.ds(k * LANES, LANES)
-        pair = block_solve(k, *s2[k], tile(y2, k, 0), tile(y2, k, 1))
-        for h in range(hb):
-            residual[h, :, at] = tile(residual, k, h) + c2 * s2[k][h]
+            residual[h, :, at] = tile(residual, k, h) + c2 * s2[h]
             precond[h, :, at] = (
-                c0 * tile(z0, k, h + 1) + c1 * tile(y1, k, h + 1) + c2 * pair[h]
+                c0 * hour(z0, h + 1, k) + c1 * hour(y1, h + 1, k) + c2 * pair[h]
             )
 
 
@@ -477,7 +548,7 @@
         and rows == SUB
         and columns == blocks * SLOT
         and pairs >= SUB
-        and pairs % 2 == 0
+        and pairs % SUB == 0
     )
     args = (observations, obs_noise, prior_noise, observed, kappa_sq, obs_precision)
     if not fits:
@@ -488,6 +559,9 @@
 
     def room(*shape):
         return pltpu.VMEM(shape, jnp.float32)
+
+    def near(x):
+        return pltpu.with_memory_space_constraint(x, pltpu.VMEM)
 
     field = shaped(hours, rows, columns)
     right, weight, chunks = pl.pallas_call(
@@ -500,21 +574,24 @@
         name="pack",
     )(*args)
     got = exchange(chunks, blocks)
+    every = pairs * hours
     chunks = pl.pallas_call(
         lambda *refs: solve_kernel(columns, *refs),
-        out_shape=pltpu.VMEM((blocks, 2, rows, LANES), jnp.float32),
-        scratch_shapes=[room(pairs * hours, rows, LANES)] * 8 + [room(pairs, rows, LANES)],
+        out_shape=pltpu.VMEM((blocks * (2 * rows - 2), LANES), jnp.float32),
+        scratch_shapes=[room(every, rows, LANES)] * 8 + [room(pairs, rows, LANES)],
         name="solve",
-    )(pltpu.with_memory_space_constraint(got, pltpu.VMEM))
-    got = lax.all_to_all(chunks, AXES, split_axis=0, concat_axis=0, tiled=True)
+    )(near(got))
+    got = exchange(chunks, blocks)
+    tiles = columns // LANES
+    flat = room(((hours + 2) * tiles + 2) * rows, LANES)
     return tuple(
         pl.pallas_call(
             unpack_kernel,
             out_shape=[field] * 3,
-            scratch_shapes=[room(hours + 2, rows, columns)] * 2
-            + [room(2, rows, columns), room(rows, columns)],
+            scratch_shapes=[flat] * 2
+            + [room(2, tiles, rows, LANES), room(tiles, rows, LANES), room(4, tiles, rows, LANES)],
             name="unpack",
-        )(*(pltpu.with_memory_space_constraint(x, pltpu.VMEM) for x in (got, right, weight, kappa_sq)))
+        )(*(near(x) for x in (got, right, weight, kappa_sq)))
     )
 
 

time: 34.1 us -> 33.4 us (0.979)
  blocking collectives: 28.6 us -> 28.1 us
    all_to_all x1 -> x0, blocking collectives: 12.4 us -> none  [per_device(): got = lax.all_to_all(chunks, AXES, split_axis=0, concat_axis=0, tiled=True)]
    all_to_all x1 -> x2, blocking collectives: 16.2 us -> 28.1 us  [exchange(): lax.all_to_all(chunks, AXES, split_axis=0, concat_axis=0, tiled=True)]
where the time goes in v5:
time: 33.4 us; the launch traced here: 33.1 us
  blocking collectives  28.1 us (84%)
  Pallas kernels  4.33 us (13%)
  between operations  0.66 us (2%)
    all_to_all x2, blocking collectives, exchange(): lax.all_to_all(chunks, AXES, split_axis=0, concat_axis=0, tiled=True)  28.1 us
    pallas_call x1, Pallas kernels, per_device(): pl.pallas_call(unpack_kernel, out_shape=[field] * 3, scratch_shapes=[flat...  1.61 us
    pallas_call x1, Pallas kernels, per_device(): pl.pallas_call(pack_kernel, out_shape=(pltpu.VMEM((hours, rows, columns),...  1.41 us
    pallas_call x1, Pallas kernels, per_device(): pl.pallas_call(lambda *refs: solve_kernel(columns, *refs), out_shape=pltp...  1.31 us

profile of v5, /device:TPU:0, one launch (start us, length us, event | category | flops | bytes accessed | tf_op | source)
XLA Modules:
  0.0 33.1 jit_solution(814025703881618303)
XLA Ops:
  0.6 1.4 %pack.1 = (f32[2,8,1024]{2,1,0:T(8,128)S(1)}, f32[2,8,1024]{2,1,0:T(8,128)S(1)}, f32[320,128]{1,0:T(8,128)S(1)}) custom-call(f32[2,8,1024]{2,1,0:T(8,128)} %obs.1, f32[2,8,1024]{2,1,0:T(8,128)} %noise.1, f32[2,8,1024]{2,1,0:T(8,128)} %prior.1, s32[2,8,1024]{2,1,0:T(8,128)} %observed.1, f32[8,1024]{1,0:T(8,128)} %kappa.3, f32[8,1024]{1,0:T(8,128)} %precision.1), custom_call_target="tpu_custom_call" | custom-call | tf_op jit(solution)/shard_map/pack/pallas_call | solution.py:567
  2.0 16.2 %all_to_all.10 = f32[32,5,2,128]{3,2,1,0:T(2,128)S(1)} all-to-all(f32[32,5,2,128]{3,2,1,0:T(2,128)S(1)} %bitcast.7), channel_id=1, replica_groups=mesh['tm'=16,'rows'=2] {'tm','rows'}, dimensions={0} | all-to-all | bytes 327680 | tf_op jit(solution)/shard_map/all_to_all | solution.py:538
  18.3 1.3 %solve.1 = f32[448,128]{1,0:T(8,128)S(1)} custom-call(f32[320,128]{1,0:T(8,128)S(1)} %bitcast.6), custom_call_target="tpu_custom_call" | custom-call | tf_op jit(solution)/shard_map/solve/pallas_call | solution.py:578
  19.6 0.0 copy-start
  19.6 11.9 %all_to_all.11 = f32[32,7,2,128]{3,2,1,0:T(2,128)S(1)} all-to-all(f32[32,7,2,128]{3,2,1,0:T(2,128)S(1)} %bitcast.5), channel_id=1, replica_groups=mesh['tm'=16,'rows'=2] {'tm','rows'}, dimensions={0} | all-to-all | bytes 458752 | tf_op jit(solution)/shard_map/all_to_all | solution.py:538
  31.5 0.0 copy-done
  31.5 1.6 %unpack.1 = (f32[2,8,1024]{2,1,0:T(8,128)}, f32[2,8,1024]{2,1,0:T(8,128)}, f32[2,8,1024]{2,1,0:T(8,128)}) custom-call(f32[448,128]{1,0:T(8,128)S(1)} %bitcast.4, f32[2,8,1024]{2,1,0:T(8,128)S(1)} %get-tuple-element.7.right, f32[2,8,1024]{2,1,0:T(8,128)S(1)} %get-tuple-element.8.weight, f32[8,1024]{1,0:T(8,128)S(1)} %copy-done), custom_call_target="tpu_custom_call" | custom-call | tf_op jit(solution)/shard_map/unpack/pallas_call | solution.py:588
Async XLA Ops:
  19.6 11.9 %copy-start = (f32[8,1024]{1,0:T(8,128)S(1)}, f32[8,1024]{1,0:T(8,128)}, u32[]{:S(2)}) copy-start(f32[8,1024]{1,0:T(8,128)} %kappa.3) | copy-start | bytes 98308

commit v6 on v5

--- a/solution.py
+++ b/solution.py
@@ -158,7 +158,7 @@
     return ref[row + (slice(None), at)] if row else ref[:, at]
 
 
-def pack_kernel(obs, noise, prior, observed, kappa, precision, right, weight, out):
+def pack_kernel(obs, noise, prior, observed, kappa, precision, pair, out):
     hours, _, columns = obs.shape
     tiles = columns // LANES
     blocks = tiles * SLOTS
@@ -171,17 +171,19 @@
     root = jnp.sqrt(prec)
     for h in range(hours):
         mask = observed[h].astype(jnp.float32)
-        right[h] = mask * (prec * obs[h] + root * noise[h]) + prior[h]
-        weight[h] = mask * prec
+        pair[0, h] = mask * (prec * obs[h] + root * noise[h]) + prior[h]
+        pair[1, h] = mask * prec
     zero = jnp.zeros((SUB, LANES), jnp.float32)
 
+    strip = lax.axis_index("rows")
     span = 2 * ITERS
     wide = 2 * hours * span
     before = lax.rem(lane // ITERS, 2) == 0
     ends, begins = [], []
     for k in range(tiles):
-        items = [tile(ref, k, h) for ref in (right, weight) for h in range(hours)]
-        for j, chunk in enumerate(quad(items, left, first)):
+        items = [tile(pair, k, i, h) for i in (0, 1) for h in range(hours)]
+        mine = [tile(pair, k, i, h) for i in (strip, 1 - strip) for h in range(hours)]
+        for j, chunk in enumerate(quad(mine, left, first)):
             out[pl.ds((k * SLOTS + j) * rows, SUB), :] = chunk
         begin, end = zero, zero
         for i, item in enumerate(items):
@@ -226,6 +228,7 @@
         halo = pltpu.roll(halo, 0, 1, stride=wide, stride_axis=0)
         halo = jnp.take_along_axis(halo, swapped, axis=0)
         halo = pltpu.roll(halo, 0, 1, stride=wide, stride_axis=0)
+        halo = jnp.where(strip == 0, halo, turn(halo, HALF))
         lines = jnp.where(
             lax.rem(sub, 2) == 0, kappa_rows(k), turn(kappa_rows(k + 1), -SLOT // 2)
         )
@@ -238,7 +241,9 @@
             out[pl.ds(block * rows + SUB + 1, 1), :] = lines[r : r + 1]
 
 
-def solve_kernel(columns, got, out, right, inv, rat, z0, y1, y2, s1, s2, side):
+def solve_kernel(
+    columns, got, out, right, inv_in, rat, z0, y1, y2, s1, s2, side, middle, totals
+):
     strips, hb = 2, 2
     rows = SUB + EXTRA
     blocks = got.shape[0] // rows
@@ -278,16 +283,13 @@
         at = pair * strips * rows
         c0, c1 = got[pl.ds(at, SUB), :], got[pl.ds(at + rows, SUB), :]
         h0, h1 = (
-            pltpu.roll(line, 0, 1, stride=wide, stride_axis=0)
-            for line in strip_rows(at + SUB)
+            pltpu.roll(line, 0, 1, stride=wide, stride_axis=0) for line in strip_rows(at + SUB)
         )
-        halo = jnp.where(left, h0, turn(h1, HALF))
+        halo = jnp.where(left, h0, h1)
+        r, w = jnp.where(left, c0, c1), jnp.where(left, c1, c0)
         result = []
-        for i, mine in enumerate(halves(c0, c1, left)):
-            for h in range(hb):
-                item = i * hb + h
-                around = turn(halo, -ITERS - item * span)
-                result.append(jnp.where(own, turn(mine, -h * SLOT), around))
+        for item, mine in enumerate((r, turn(r, -SLOT), turn(w, HALF), turn(w, SLOT))):
+            result.append(jnp.where(own, mine, turn(halo, -ITERS - item * span)))
         return result
 
     def hour_weight(t):
@@ -305,20 +307,28 @@
         for t, r, iv in zip(hours, rhs, (inv_a, inv_b)):
             c = off * iv
             g = r * iv if g is None else r * iv - c * g
-            right[t], inv[t], rat[t], z0[t] = r, iv, c, g
+            right[t], rat[t], z0[t] = r, c, g
+            inv_in[t] = jnp.where(inside, coupling * iv, 0.0)
         return inv_b, g
 
-    upper = lower = None
-    for i in range(0, half, hb):
-        r_a, r_b, w_a, w_b = fields(i // hb)
-        q_a, q_b, v_a, v_b = fields(pairs - 1 - i // hb)
-        upper = eliminate((i, i + 1), (r_a, r_b), (w_a, w_b), upper)
-        lower = eliminate((every - 1 - i, every - 2 - i), (q_b, q_a), (v_b, v_a), lower)
     top, low_t = half - 1, half
-    joint = 1.0 / (1.0 - rat[top] * rat[low_t])
+
+    def phase(body):
+        pl.when(block >= 0)(body)
+
+    @phase
+    def _():
+        upper = lower = None
+        for i in range(0, half, hb):
+            r_a, r_b, w_a, w_b = fields(i // hb)
+            q_a, q_b, v_a, v_b = fields(pairs - 1 - i // hb)
+            upper = eliminate((i, i + 1), (r_a, r_b), (w_a, w_b), upper)
+            lower = eliminate((every - 1 - i, every - 2 - i), (q_b, q_a), (v_b, v_a), lower)
+        middle[...] = 1.0 / (1.0 - rat[top] * rat[low_t])
+
 
     def outward(ref):
-        a = (ref[top] - rat[top] * ref[low_t]) * joint
+        a = (ref[top] - rat[top] * ref[low_t]) * middle[...]
         b = ref[low_t] - rat[low_t] * a
         ref[top], ref[low_t] = a, b
         for i in range(1, half):
@@ -330,56 +340,29 @@
         a = b = None
         for i in range(half):
             j = every - 1 - i
-            a = source[i] * inv[i] if a is None else source[i] * inv[i] - rat[i] * a
-            b = source[j] * inv[j] if b is None else source[j] * inv[j] - rat[j] * b
+            a = source[i] * inv_in[i] if a is None else source[i] * inv_in[i] - rat[i] * a
+            b = source[j] * inv_in[j] if b is None else source[j] * inv_in[j] - rat[j] * b
             ref[i], ref[j] = a, b
 
     last, initial = sub == SUB - 1, sub == 0
     edge = (last & ~low) | (initial & low)
-    low_row = low[:1]
 
     def beside(v, t, base):
         across = jnp.where(edge, turn(v, HALF), 0.0)
-        line = jnp.where(low_row, across[:1], across[SUB - 1 :])
         pair, h = divmod(t, hb)
-        side[pair, base + 1 + h : base + 2 + h] = line
-        other, spot = (pair - 1, hb + 1) if h == 0 else (pair + 1, 0)
-        if 0 <= other < pairs:
-            side[other, base + spot : base + spot + 1] = line
+        for i, row in enumerate((0, SUB - 1)):
+            side[i, pair, base + h : base + h + 1] = across[row : row + 1]
         up = pltpu.roll(jnp.where(last, across, v), 1, 0)
         down = pltpu.roll(jnp.where(initial, across, v), SUB - 1, 0)
         return (up + down) + (turn(v, 1) + turn(v, -1))
 
     def split(ref, result, base):
-        old, now = zero, beside(ref[0], 0, base)
+        old, now = zero, ref[0]
         for t in range(every):
-            new = beside(ref[t + 1], t + 1, base) if t + 1 < every else zero
-            value = hour_weight(t) * now - coupling * (old + new)
-            result[t] = jnp.where(inside, value, 0.0)
+            new = ref[t + 1] if t + 1 < every else zero
+            mixed = (hour_weight(t) / coupling) * now - (old + new)
+            result[t] = beside(mixed, t, base)
             old, now = now, new
-
-    side[0], side[pairs - 1] = zero, zero
-    outward(z0)
-    split(z0, s1, 0)
-    inward(s1, y1)
-    outward(y1)
-    split(y1, s2, hb + 2)
-    inward(s2, y2)
-    outward(y2)
-
-    totals = [zero, zero]
-    products = ((right, z0), (z0, s1), (right, y1), (s1, y1), (z0, s2), (y1, s2))
-    for i, (x, y) in enumerate(products):
-        parts = [x[t] * y[t] for t in range(4)]
-        for t in range(4, every):
-            parts[t % 4] = parts[t % 4] + x[t] * y[t]
-        part = jnp.where(own, (parts[0] + parts[1]) + (parts[2] + parts[3]), 0.0)
-        part = jnp.sum(part, axis=0, keepdims=True)
-        totals[i // 3] = jnp.where(sub == i % 3 + 2, part, totals[i // 3])
-    totals = [part + turn(part, HALF) for part in totals]
-    totals = [part + turn(part, -SLOT // 2) for part in totals]
-    low_part = lax.rem(lane, SLOT) < SLOT // 2
-    total = jnp.where(low_part, turn(totals[0], SLOT), turn(totals[1], SLOT + SLOT // 2))
 
     def two(ref, pair):
         before = ref[pair * hb - 1] if pair > 0 else zero
@@ -387,36 +370,69 @@
         return jnp.where(first, before, turn(after, SLOT))
 
     size = out.shape[0] // blocks
-    inner_w = 1.0 + coupling * coupling
-    hour_row = lax.rem(sub, hb + 2)
-
-    def edge_rows(pair):
-        lines = side[pair]
-        weight = inner_w
-        if pair == 0:
-            weight = jnp.where(hour_row == 0, 1.0, inner_w)
-        if pair == pairs - 1:
-            weight = jnp.where(hour_row == 1, 1.0, inner_w)
-        around = lines + pltpu.roll(lines, SUB - 2, 0)
-        added = weight * pltpu.roll(lines, SUB - 1, 0) - coupling * around
-        return jnp.where(sub < 4, pltpu.roll(added, 2, 0), added)
-
+
+    def shared(a, b):
+        b = turn(b, HALF)
+        return jnp.where(left, a, b), jnp.where(left, b, a)
+
+    def total_of(i, x, y):
+        parts = [x[t] * y[t] for t in range(4)]
+        for t in range(4, every):
+            parts[t % 4] = parts[t % 4] + x[t] * y[t]
+        totals[i] = (parts[0] + parts[1]) + (parts[2] + parts[3])
+
+    @phase
+    def _():
+        outward(z0)
+
+    @phase
+    def _():
+        split(z0, s1, 2)
+        total_of(0, right, z0)
+
+    @phase
+    def _():
+        inward(s1, y1)
+        outward(y1)
+
+    @phase
+    def _():
+        split(y1, s2, 4)
+        total_of(1, z0, s1)
+        total_of(2, right, y1)
+        total_of(3, s1, y1)
+
+    @phase
+    def _():
+        inward(s2, y2)
+        outward(y2)
+        total_of(4, z0, s2)
+        total_of(5, y1, s2)
+        sums = [zero, zero]
+        for i in range(6):
+            part = jnp.sum(jnp.where(own, totals[i], 0.0), axis=0, keepdims=True)
+            part = part * (1.0 if i in (0, 2) else coupling)
+            sums[i // 3] = jnp.where(sub == i % 3 + 2, part, sums[i // 3])
+        sums = [part + turn(part, HALF) for part in sums]
+        sums = [part + turn(part, -SLOT // 2) for part in sums]
+        low_part = lax.rem(lane, SLOT) < SLOT // 2
+        middle[...] = jnp.where(low_part, turn(sums[0], SLOT), turn(sums[1], SLOT + SLOT // 2))
+        for pair in range(pairs):
+            for strip, chunk in enumerate(shared(two(z0, pair), two(y1, pair))):
+                out[pl.ds((strips * pair + strip) * size, SUB), :] = chunk
+
+    total = middle[...]
     for pair in range(pairs):
         mine = two(y2, pair)
-        other = jnp.where(first, edge_rows(pair), total)
+        line = jnp.where(low, side[0, pair], side[1, pair]) * coupling
+        other = jnp.where(first, line, total)
         other = jnp.where(sub >= SUB - 2, mine, other)
-        for strip, chunk in enumerate(halves(pltpu.roll(mine, 2, 0), other, left)):
-            out[pl.ds((strips * pair + strip) * size + SUB - 2, SUB), :] = chunk
-        for strip, chunk in enumerate(halves(two(z0, pair), two(y1, pair), left)):
-            out[pl.ds((strips * pair + strip) * size, SUB), :] = chunk
-
-
-def at_hour(t, rows=SUB, shift=0):
-    return pl.ds((t + 1) * SUB + shift, rows)
+        for strip, chunk in enumerate(shared(pltpu.roll(mine, 2, 0), other)):
+            out[pl.ds((strips * pair + strip) * size + SUB, SUB - 2), :] = chunk[2:]
 
 
 def unpack_kernel(
-    got, right, weight, kappa, solution, residual, precond, z0, y1, y2, side, coef
+    got, pair, kappa, solution, residual, precond, zy, y2, side, coef
 ):
     hb = 2
     size = 2 * SUB - 2
@@ -433,8 +449,8 @@
     for k in range(tiles):
         diag = tile(kappa, k) + 4.0
         off = -coupling * diag
-        d_a = e_a * diag + tile(weight, k, 0)
-        d_b = e_b * diag + tile(weight, k, 1)
+        d_a = e_a * diag + tile(pair, k, 1, 0)
+        d_b = e_b * diag + tile(pair, k, 1, 1)
         scale = 1.0 / (d_a * d_b - off * off)
         coef[0, k], coef[1, k], coef[2, k], coef[3, k] = d_b * scale, off * scale, d_a * scale, off
 
@@ -444,8 +460,8 @@
     def late_of(c):
         return got[pl.ds(c * size + SUB - 2, SUB), :]
 
-    def spot(q, k):
-        return q * tiles + k
+    def spot(field, q, k):
+        return (field * (hb + 2) + q) * tiles + k
 
     parts = [late_of(c) for c in range(4)]
     for c in range(4, blocks):
@@ -453,7 +469,7 @@
     total = (parts[0] + parts[1]) + (parts[2] + parts[3])
     sums = []
     for i in range(2):
-        begin = LANES - SLOT + i * (SLOT // 2)
+        begin = jnp.where(strip == 0, LANES - SLOT, SLOT) + i * (SLOT // 2)
         here = (lane >= begin) & (lane < begin + SLOT // 2)
         part = jnp.sum(jnp.where(here, total, 0.0), axis=1, keepdims=True)
         part = jnp.broadcast_to(part, (SUB, LANES))
@@ -463,10 +479,12 @@
     for k in range(tiles):
         group = range(k * SLOTS, k * SLOTS + SLOTS)
         early = quad([early_of(c) for c in group], left, first)
-        for ref, b, a in ((z0, early[0], early[1]), (y1, early[2], early[3])):
-            ref[at_hour(spot(0, k)), :], ref[at_hour(spot(hb + 1, k)), :] = b, a
+        for field, b, a in ((strip, early[0], early[1]), (1 - strip, early[2], early[3])):
+            zy[spot(field, 0, k)], zy[spot(field, hb + 1, k)] = b, a
         q = [late_of(c) for c in group]
         (p0, p2), (p1, p3) = halves(q[0], q[2], left), halves(q[1], q[3], left)
+        p0, p2 = jnp.where(strip == 0, p0, p2), jnp.where(strip == 0, p2, p0)
+        p1, p3 = jnp.where(strip == 0, p1, p3), jnp.where(strip == 0, p3, p1)
         p0, p1 = (
             jnp.where(sub < SUB - 2, pltpu.roll(p, SUB - 2, 0), high)
             for p, high in ((p0, p2), (p1, p3))
@@ -482,53 +500,50 @@
         f_a, f_b = f_a - coef[3, k] * before, f_b - coef[3, k] * after
         return coef[0, k] * f_a - coef[1, k] * f_b, coef[2, k] * f_b - coef[1, k] * f_a
 
-    quarter = range(hb + 2)
-
-    def split(ref, base):
-        passed = [0.0] * (hb + 2)
-        back = [turn(ref[at_hour(spot(q, 0)), :], -1) for q in quarter]
+    def split(field, base):
+        def mixed(k):
+            v = [zy[spot(field, q, k)] for q in range(hb + 2)]
+            combined = [
+                e * v[h + 1] - coupling * (v[h] + v[h + 2]) for h, e in enumerate((e_a, e_b))
+            ]
+            return [(c, turn(c, 1), turn(c, -1)) for c in combined]
+
+        before, now = [(0.0, 0.0, 0.0)] * hb, mixed(0)
         for k in range(tiles):
-            forward = [turn(ref[at_hour(spot(q, k)), :], 1) for q in quarter]
-            more = k + 1 < tiles
-            coming = [
-                turn(ref[at_hour(spot(q, k + 1)), :], -1) if more else 0.0 for q in quarter
-            ]
-            near = []
-            for q in quarter:
-                v = ref[at_hour(spot(q, k)), :]
-                up = pltpu.roll(jnp.where(last, 0.0, v), 1, 0)
-                down = pltpu.roll(jnp.where(initial, 0.0, v), SUB - 1, 0)
-                west = jnp.where(lane == 0, passed[q], forward[q])
-                east = jnp.where(lane == LANES - 1, coming[q], back[q])
-                near.append((up + down) + (east + west))
+            after = mixed(k + 1) if k + 1 < tiles else [(0.0, 0.0, 0.0)] * hb
             result = []
-            for h, e in enumerate((e_a, e_b)):
+            for h in range(hb):
+                c, forward, back = now[h]
+                up = pltpu.roll(jnp.where(last, 0.0, c), 1, 0)
+                down = pltpu.roll(jnp.where(initial, 0.0, c), SUB - 1, 0)
+                west = jnp.where(lane == 0, before[h][1], forward)
+                east = jnp.where(lane == LANES - 1, after[h][2], back)
                 line = jnp.where(edge, side[k, base + h : base + h + 1, :], 0.0)
-                result.append(e * near[h + 1] - coupling * (near[h] + near[h + 2]) + line)
+                result.append((up + down) + (east + west) + line)
             yield k, *result
-            passed, back = forward, coming
-
-    def hour(ref, q, k):
-        return ref[at_hour(spot(q, k)), :]
+            before, now = now, after
+
+    def hour(field, q, k):
+        return zy[spot(field, q, k)]
 
     for k in range(tiles):
-        z0[at_hour(spot(1, k)), :], z0[at_hour(spot(2, k)), :] = block_solve(
-            k, tile(right, k, 0), tile(right, k, 1), hour(z0, 0, k), hour(z0, 3, k)
+        zy[spot(0, 1, k)], zy[spot(0, 2, k)] = block_solve(
+            k, tile(pair, k, 0, 0), tile(pair, k, 0, 1), hour(0, 0, k), hour(0, 3, k)
         )
-    for k, *s1 in split(z0, 2):
+    for k, *s1 in split(0, 2):
         at = pl.ds(k * LANES, LANES)
-        pair = block_solve(k, *s1, hour(y1, 0, k), hour(y1, 3, k))
+        solved = block_solve(k, *s1, hour(1, 0, k), hour(1, 3, k))
         for h in range(hb):
-            y1[at_hour(spot(h + 1, k)), :] = pair[h]
-            solution[h, :, at] = cx * hour(z0, h + 1, k) + c2 * pair[h]
-            residual[h, :, at] = c0 * tile(right, k, h) + c1 * s1[h]
-    for k, *s2 in split(y1, 4):
+            zy[spot(1, h + 1, k)] = solved[h]
+            solution[h, :, at] = cx * hour(0, h + 1, k) + c2 * solved[h]
+            residual[h, :, at] = c0 * tile(pair, k, 0, h) + c1 * s1[h]
+    for k, *s2 in split(1, 4):
         at = pl.ds(k * LANES, LANES)
-        pair = block_solve(k, *s2, y2[0, k], y2[1, k])
+        solved = block_solve(k, *s2, y2[0, k], y2[1, k])
         for h in range(hb):
             residual[h, :, at] = tile(residual, k, h) + c2 * s2[h]
             precond[h, :, at] = (
-                c0 * hour(z0, h + 1, k) + c1 * hour(y1, h + 1, k) + c2 * pair[h]
+                c0 * hour(0, h + 1, k) + c1 * hour(1, h + 1, k) + c2 * solved[h]
             )
 
 
@@ -564,11 +579,10 @@
         return pltpu.with_memory_space_constraint(x, pltpu.VMEM)
 
     field = shaped(hours, rows, columns)
-    right, weight, chunks = pl.pallas_call(
+    pair, chunks = pl.pallas_call(
         pack_kernel,
         out_shape=(
-            pltpu.VMEM((hours, rows, columns), jnp.float32),
-            pltpu.VMEM((hours, rows, columns), jnp.float32),
+            pltpu.VMEM((2, hours, rows, columns), jnp.float32),
             pltpu.VMEM((blocks * (rows + EXTRA), LANES), jnp.float32),
         ),
         name="pack",
@@ -578,20 +592,23 @@
     chunks = pl.pallas_call(
         lambda *refs: solve_kernel(columns, *refs),
         out_shape=pltpu.VMEM((blocks * (2 * rows - 2), LANES), jnp.float32),
-        scratch_shapes=[room(every, rows, LANES)] * 8 + [room(pairs, rows, LANES)],
+        scratch_shapes=[room(every, rows, LANES)] * 8 + [room(2, pairs, rows, LANES), room(rows, LANES), room(6, rows, LANES)],
         name="solve",
     )(near(got))
     got = exchange(chunks, blocks)
     tiles = columns // LANES
-    flat = room(((hours + 2) * tiles + 2) * rows, LANES)
     return tuple(
         pl.pallas_call(
             unpack_kernel,
             out_shape=[field] * 3,
-            scratch_shapes=[flat] * 2
-            + [room(2, tiles, rows, LANES), room(tiles, rows, LANES), room(4, tiles, rows, LANES)],
+            scratch_shapes=[
+                room(2 * (hours + 2) * tiles, rows, LANES),
+                room(2, tiles, rows, LANES),
+                room(tiles, rows, LANES),
+                room(4, tiles, rows, LANES),
+            ],
             name="unpack",
-        )(*(near(x) for x in (got, right, weight, kappa_sq)))
+        )(*(near(x) for x in (got, pair, kappa_sq)))
     )
 
 

time: 33.4 us -> 32.7 us (0.979)
  Pallas kernels: 4.33 us -> 3.68 us
    pallas_call x2, Pallas kernels: 3.02 us -> 2.58 us  [the longest x1 1.47 us: per_device(): pl.pallas_call(pack_kernel, out_shape=(pltpu.VMEM((2, hours, rows, column...]
where the time goes in v6:
time: 32.7 us; the launch traced here: 32.5 us
  blocking collectives  28.1 us (86%)
  Pallas kernels  3.68 us (11%)
  between operations  0.66 us (2%)
    all_to_all x2, blocking collectives, exchange(): lax.all_to_all(chunks, AXES, split_axis=0, concat_axis=0, tiled=True)  28.1 us
    pallas_call x1, Pallas kernels, per_device(): pl.pallas_call(pack_kernel, out_shape=(pltpu.VMEM((2, hours, rows, column...  1.47 us
    pallas_call x1, Pallas kernels, per_device(): pl.pallas_call(unpack_kernel, out_shape=[field] * 3, scratch_shapes=[room...  1.11 us
    pallas_call x1, Pallas kernels, per_device(): pl.pallas_call(lambda *refs: solve_kernel(columns, *refs), out_shape=pltp...  1.1 us

profile of v6, /device:TPU:0, one launch (start us, length us, event | category | flops | bytes accessed | tf_op | source)
XLA Modules:
  0.0 32.5 jit_solution(11001493251232412714)
XLA Ops:
  0.6 1.5 %pack.1 = (f32[2,2,8,1024]{3,2,1,0:T(8,128)S(1)}, f32[320,128]{1,0:T(8,128)S(1)}) custom-call(f32[2,8,1024]{2,1,0:T(8,128)} %obs.1, f32[2,8,1024]{2,1,0:T(8,128)} %noise.1, f32[2,8,1024]{2,1,0:T(8,128)} %prior.1, s32[2,8,1024]{2,1,0:T(8,128)} %observed.1, f32[8,1024]{1,0:T(8,128)} %kappa.3, f32[8,1024]{1,0:T(8,128)} %precision.1), custom_call_target="tpu_custom_call" | custom-call | tf_op jit(solution)/shard_map/pack/pallas_call | solution.py:582
  2.1 16.2 %all_to_all.10 = f32[32,5,2,128]{3,2,1,0:T(2,128)S(1)} all-to-all(f32[32,5,2,128]{3,2,1,0:T(2,128)S(1)} %bitcast.7), channel_id=1, replica_groups=mesh['tm'=16,'rows'=2] {'tm','rows'}, dimensions={0} | all-to-all | bytes 327680 | tf_op jit(solution)/shard_map/all_to_all | solution.py:553
  18.4 1.1 %solve.1 = f32[448,128]{1,0:T(8,128)S(1)} custom-call(f32[320,128]{1,0:T(8,128)S(1)} %bitcast.6), custom_call_target="tpu_custom_call" | custom-call | tf_op jit(solution)/shard_map/solve/pallas_call | solution.py:592
  19.5 0.0 copy-start
  19.5 11.9 %all_to_all.11 = f32[32,7,2,128]{3,2,1,0:T(2,128)S(1)} all-to-all(f32[32,7,2,128]{3,2,1,0:T(2,128)S(1)} %bitcast.5), channel_id=1, replica_groups=mesh['tm'=16,'rows'=2] {'tm','rows'}, dimensions={0} | all-to-all | bytes 458752 | tf_op jit(solution)/shard_map/all_to_all | solution.py:553
  31.3 0.0 copy-done
  31.3 1.1 %unpack.1 = (f32[2,8,1024]{2,1,0:T(8,128)}, f32[2,8,1024]{2,1,0:T(8,128)}, f32[2,8,1024]{2,1,0:T(8,128)}) custom-call(f32[448,128]{1,0:T(8,128)S(1)} %bitcast.4, f32[2,2,8,1024]{3,2,1,0:T(8,128)S(1)} %get-tuple-element.6.pair, f32[8,1024]{1,0:T(8,128)S(1)} %copy-done), custom_call_target="tpu_custom_call" | custom-call | tf_op jit(solution)/shard_map/unpack/pallas_call | solution.py:601
Async XLA Ops:
  19.5 11.9 %copy-start = (f32[8,1024]{1,0:T(8,128)S(1)}, f32[8,1024]{1,0:T(8,128)}, u32[]{:S(2)}) copy-start(f32[8,1024]{1,0:T(8,128)} %kappa.3) | copy-start | bytes 98308

commit v7 on v6

--- a/solution.py
+++ b/solution.py
@@ -182,7 +182,10 @@
     ends, begins = [], []
     for k in range(tiles):
         items = [tile(pair, k, i, h) for i in (0, 1) for h in range(hours)]
-        mine = [tile(pair, k, i, h) for i in (strip, 1 - strip) for h in range(hours)]
+        mine = [
+            jnp.where(strip == 0, items[i], items[(i + hours) % (2 * hours)])
+            for i in range(2 * hours)
+        ]
         for j, chunk in enumerate(quad(mine, left, first)):
             out[pl.ds((k * SLOTS + j) * rows, SUB), :] = chunk
         begin, end = zero, zero
@@ -216,7 +219,7 @@
             (sub // 2 == 1) & (lane < HALF), kap[min(k + 1, tiles - 1)], here
         )
 
-    falling = lax.rem(SUB - sub, SUB)
+    falling = lax.rem(SUB - sub + strip * (SUB // 2), SUB)
     swapped = lax.rem(lane // wide + sub, SUB)
     for k in range(0, tiles, 2):
         near = [
@@ -228,7 +231,6 @@
         halo = pltpu.roll(halo, 0, 1, stride=wide, stride_axis=0)
         halo = jnp.take_along_axis(halo, swapped, axis=0)
         halo = pltpu.roll(halo, 0, 1, stride=wide, stride_axis=0)
-        halo = jnp.where(strip == 0, halo, turn(halo, HALF))
         lines = jnp.where(
             lax.rem(sub, 2) == 0, kappa_rows(k), turn(kappa_rows(k + 1), -SLOT // 2)
         )
@@ -404,6 +406,9 @@
 
     @phase
     def _():
+        for pair in range(pairs):
+            for strip, chunk in enumerate(shared(two(z0, pair), two(y1, pair))):
+                out[pl.ds((strips * pair + strip) * size, SUB), :] = chunk
         inward(s2, y2)
         outward(y2)
         total_of(4, z0, s2)
@@ -417,9 +422,6 @@
         sums = [part + turn(part, -SLOT // 2) for part in sums]
         low_part = lax.rem(lane, SLOT) < SLOT // 2
         middle[...] = jnp.where(low_part, turn(sums[0], SLOT), turn(sums[1], SLOT + SLOT // 2))
-        for pair in range(pairs):
-            for strip, chunk in enumerate(shared(two(z0, pair), two(y1, pair))):
-                out[pl.ds((strips * pair + strip) * size, SUB), :] = chunk
 
     total = middle[...]
     for pair in range(pairs):

time: 32.7 us -> 32.6 us (level)
  no operation moved by 1% of the time
where the time goes in v7:
time: 32.6 us; the launch traced here: 32.4 us
  blocking collectives  28.1 us (86%)
  Pallas kernels  3.62 us (11%)
  between operations  0.66 us (2%)
    all_to_all x2, blocking collectives, exchange(): lax.all_to_all(chunks, AXES, split_axis=0, concat_axis=0, tiled=True)  28.1 us
    pallas_call x1, Pallas kernels, per_device(): pl.pallas_call(pack_kernel, out_shape=(pltpu.VMEM((2, hours, rows, column...  1.41 us
    pallas_call x1, Pallas kernels, per_device(): pl.pallas_call(unpack_kernel, out_shape=[field] * 3, scratch_shapes=[room...  1.11 us
    pallas_call x1, Pallas kernels, per_device(): pl.pallas_call(lambda *refs: solve_kernel(columns, *refs), out_shape=pltp...  1.1 us

profile of v7, /device:TPU:0, one launch (start us, length us, event | category | flops | bytes accessed | tf_op | source)
XLA Modules:
  0.0 32.4 jit_solution(9042261420440259220)
XLA Ops:
  0.6 1.4 %pack.1 = (f32[2,2,8,1024]{3,2,1,0:T(8,128)S(1)}, f32[320,128]{1,0:T(8,128)S(1)}) custom-call(f32[2,8,1024]{2,1,0:T(8,128)} %obs.1, f32[2,8,1024]{2,1,0:T(8,128)} %noise.1, f32[2,8,1024]{2,1,0:T(8,128)} %prior.1, s32[2,8,1024]{2,1,0:T(8,128)} %observed.1, f32[8,1024]{1,0:T(8,128)} %kappa.3, f32[8,1024]{1,0:T(8,128)} %precision.1), custom_call_target="tpu_custom_call" | custom-call | tf_op jit(solution)/shard_map/pack/pallas_call | solution.py:584
  2.0 16.2 %all_to_all.10 = f32[32,5,2,128]{3,2,1,0:T(2,128)S(1)} all-to-all(f32[32,5,2,128]{3,2,1,0:T(2,128)S(1)} %bitcast.7), channel_id=1, replica_groups=mesh['tm'=16,'rows'=2] {'tm','rows'}, dimensions={0} | all-to-all | bytes 327680 | tf_op jit(solution)/shard_map/all_to_all | solution.py:555
  18.3 1.1 %solve.1 = f32[448,128]{1,0:T(8,128)S(1)} custom-call(f32[320,128]{1,0:T(8,128)S(1)} %bitcast.6), custom_call_target="tpu_custom_call" | custom-call | tf_op jit(solution)/shard_map/solve/pallas_call | solution.py:594
  19.4 0.0 copy-start
  19.4 11.9 %all_to_all.11 = f32[32,7,2,128]{3,2,1,0:T(2,128)S(1)} all-to-all(f32[32,7,2,128]{3,2,1,0:T(2,128)S(1)} %bitcast.5), channel_id=1, replica_groups=mesh['tm'=16,'rows'=2] {'tm','rows'}, dimensions={0} | all-to-all | bytes 458752 | tf_op jit(solution)/shard_map/all_to_all | solution.py:555
  31.3 0.0 copy-done
  31.3 1.1 %unpack.1 = (f32[2,8,1024]{2,1,0:T(8,128)}, f32[2,8,1024]{2,1,0:T(8,128)}, f32[2,8,1024]{2,1,0:T(8,128)}) custom-call(f32[448,128]{1,0:T(8,128)S(1)} %bitcast.4, f32[2,2,8,1024]{3,2,1,0:T(8,128)S(1)} %get-tuple-element.6.pair, f32[8,1024]{1,0:T(8,128)S(1)} %copy-done), custom_call_target="tpu_custom_call" | custom-call | tf_op jit(solution)/shard_map/unpack/pallas_call | solution.py:603
Async XLA Ops:
  19.4 11.9 %copy-start = (f32[8,1024]{1,0:T(8,128)S(1)}, f32[8,1024]{1,0:T(8,128)}, u32[]{:S(2)}) copy-start(f32[8,1024]{1,0:T(8,128)} %kappa.3) | copy-start | bytes 98308
